TPU v7x, 32 devices: a whole 2x2x4 slice. The times are simulated.
32 devices in a mesh: seq: 8 (over z, x), ch: 4 (over y, core).
Axes of the slice: x: 2, y: 2, z: 4, core: 2. Of those that a mesh axis runs over, the one named last changes fastest.
Arguments:
- block_input: bfloat16 [131072, 2048], P('seq', 'ch'), may hold values from -6 to 6
- gate_pre: bfloat16 [131072, 2048], P('seq', 'ch'), may hold values from -8 to 8
- out_grad: bfloat16 [131072, 2048], P('seq', 'ch'), may hold values from -6 to 6
- block_weight: bfloat16 [256, 512, 512], P('seq', 'ch'), may hold values from -0.25 to 0.25
- offset_weight: bfloat16 [512, 256, 256], P(('seq', 'ch')), may hold values from -0.375 to 0.375
- out_weight: bfloat16 [2048, 2048], P(None, 'ch'), may hold values from -0.125 to 0.125
- reset_offset: int32 [256], replicated, may hold values from 0 to 512, as said below
Outputs:
- input_grad: bfloat16 [131072, 2048], P('seq', 'ch')
- gate_grad: bfloat16 [131072, 2048], P('seq', 'ch')
- block_grad: bfloat16 [256, 512, 512], P('seq', 'ch')
- offset_grad: bfloat16 [512, 256, 256], P(('seq', 'ch'))
- out_weight_grad: bfloat16 [2048, 2048], P('seq', 'ch')
Inputs may be any that keep to these rules, and one draw needn't show every extreme that they name: reset_offset[0] is 0 and the last block starts no document; other blocks start a document at some place or none.
All inputs are finite; a program needn't handle non-finite values.
Results may differ from a plain program's by a relative error of at most 0.013.
Values may be sent and summed in bfloat16 or wider, within the bound.
No kernel may reach another device: no remote copies, remote signals or barrier semaphores. Data moves between devices by JAX's collectives and lax.ppermute only.
A program may use at most 512 MiB of HBM per device.

v0:
```python
import jax
import jax.numpy as jnp
from jax import lax
from jax.sharding import PartitionSpec as P


def side_flags_of(reset_offset, block_span):
    within = jnp.arange(block_span, dtype=jnp.int32)
    return within[None, :] >= reset_offset[:, None]


def document_ids(reset_offset, block_span):
    starts = (reset_offset < block_span).astype(jnp.int32)
    earlier = jnp.cumsum(starts) - starts
    return earlier[:, None] + side_flags_of(reset_offset, block_span).astype(jnp.int32)


def to_offsets(blocked, seq_count, ch_count):
    block_count, block_span, channels = blocked.shape
    arrived = lax.all_to_all(
        blocked.reshape(1, block_count, block_span, channels),
        ("seq", "ch"),
        split_axis=2,
        concat_axis=0,
        tiled=True,
    )
    return arrived.reshape(
        seq_count, ch_count, block_count, block_span // (seq_count * ch_count), channels
    )


def to_blocks(spread, seq_count, ch_count):
    block_count = spread.shape[2]
    offsets = spread.shape[3]
    channels = spread.shape[4]
    arrived = lax.all_to_all(
        spread.reshape(seq_count * ch_count, block_count, offsets, channels),
        ("seq", "ch"),
        split_axis=0,
        concat_axis=2,
        tiled=True,
    )
    return arrived.reshape(block_count, offsets * seq_count * ch_count, channels)


def on_device(
    block_input, gate_pre, out_grad, block_weight, offset_weight, out_weight, reset_offset
):
    seq_count = lax.axis_size("seq")
    ch_count = lax.axis_size("ch")
    token_count, channels = block_input.shape
    block_span = block_weight.shape[2]
    block_count = token_count // block_span
    offsets = block_span // (seq_count * ch_count)
    full_grad, full_weight = (
        lax.all_gather(out_grad, "ch", axis=1, tiled=True),
        lax.all_gather(block_weight, "ch", axis=1, tiled=True),
    )
    seq_index = lax.axis_index("seq")
    flat_index = seq_index * ch_count + lax.axis_index("ch")
    side_table = side_flags_of(reset_offset, block_span)
    doc_table = document_ids(reset_offset, block_span)
    total_blocks = doc_table.shape[0]
    local_sides = lax.dynamic_slice_in_dim(side_table, seq_index * block_count, block_count, 0)
    mask_one = local_sides[:, :, None] == local_sides[:, None, :]
    masked_one = jnp.where(mask_one, full_weight, jnp.zeros_like(full_weight))
    inputs = block_input.reshape(block_count, block_span, channels)
    section_out = jnp.einsum(
        "ikj,ijd->ikd", masked_one, inputs, preferred_element_type=jnp.float32
    ).astype(jnp.bfloat16)
    section_spread = to_offsets(section_out, seq_count, ch_count)
    labels = lax.dynamic_slice_in_dim(doc_table, flat_index * offsets, offsets, 1).T
    mask_two = labels[:, :, None] == labels[:, None, :]
    masked_two = jnp.where(mask_two, offset_weight, jnp.zeros_like(offset_weight))
    masked_two = masked_two.reshape(offsets, seq_count, block_count, seq_count, block_count)
    mixer_spread = jnp.einsum(
        "kpqsi,scikd->pcqkd", masked_two, section_spread, preferred_element_type=jnp.float32
    ).astype(jnp.bfloat16)
    mixer_out = to_blocks(mixer_spread, seq_count, ch_count).reshape(token_count, channels)
    head_grad = jnp.dot(full_grad, out_weight, preferred_element_type=jnp.float32)
    sigmoid_gate = jax.nn.sigmoid(gate_pre.astype(jnp.float32))
    mixer_float = mixer_out.astype(jnp.float32)
    gated_out = (mixer_float * sigmoid_gate).astype(jnp.bfloat16)
    weight_share = lax.psum_scatter(
        jnp.einsum("te,tc->ec", full_grad, gated_out, preferred_element_type=jnp.float32).astype(
            jnp.bfloat16
        ),
        "seq",
        scatter_dimension=0,
        tiled=True,
    )
    mixer_grad = (head_grad * sigmoid_gate).astype(jnp.bfloat16)
    gate_grad = (head_grad * mixer_float * sigmoid_gate * (1.0 - sigmoid_gate)).astype(jnp.bfloat16)
    grad_spread = to_offsets(
        mixer_grad.reshape(block_count, block_span, channels), seq_count, ch_count
    )
    offset_grad = jnp.einsum(
        "pcqkd,scikd->kpqsi", grad_spread, section_spread, preferred_element_type=jnp.float32
    ).reshape(offsets, total_blocks, total_blocks)
    section_grad_spread = jnp.einsum(
        "kpqsi,pcqkd->scikd", masked_two, grad_spread, preferred_element_type=jnp.float32
    ).astype(jnp.bfloat16)
    offset_grad = jnp.where(mask_two, offset_grad, jnp.zeros_like(offset_grad)).astype(jnp.bfloat16)
    section_grad = to_blocks(section_grad_spread, seq_count, ch_count)
    partial_grad = jnp.einsum(
        "ikd,ijd->ikj", section_grad, inputs, preferred_element_type=jnp.float32
    )
    partial_grad = jnp.where(mask_one, partial_grad, jnp.zeros_like(partial_grad))
    block_grad = lax.psum_scatter(
        partial_grad.astype(jnp.bfloat16), "ch", scatter_dimension=1, tiled=True
    )
    input_grad = jnp.einsum(
        "ikj,ikd->ijd", masked_one, section_grad, preferred_element_type=jnp.float32
    ).astype(jnp.bfloat16)
    return (
        input_grad.reshape(token_count, channels),
        gate_grad,
        block_grad,
        offset_grad,
        weight_share,
    )


def solution(mesh):
    in_specs = (
        P("seq", "ch"),
        P("seq", "ch"),
        P("seq", "ch"),
        P("seq", "ch", None),
        P(("seq", "ch"), None, None),
        P(None, "ch"),
        P(),
    )
    out_specs = (
        P("seq", "ch"),
        P("seq", "ch"),
        P("seq", "ch", None),
        P(("seq", "ch"), None, None),
        P("seq", "ch"),
    )
    return jax.shard_map(
        on_device, mesh=mesh, in_specs=in_specs, out_specs=out_specs, check_vma=False
    )
```

profile of v0, /device:TPU:6, one launch (start us, length us, event | category | flops | bytes accessed | tf_op | source)
XLA Modules:
  0.0 2105.8 jit_solution(565953672333166698)
XLA Ops:
  7.2 0.0 copy-start
  7.2 0.0 copy-start.6
  7.2 0.0 all-gather.3.cloned.1.call-start
  7.2 0.7 all-gather.3.cloned.1.call-update
  7.9 0.0 all-gather.5.cloned.1.call-start
  8.0 0.7 all-gather.5.cloned.1.call-update
  8.7 0.0 copy-done.6
  8.7 0.1 iota_compare_fusion
  8.9 0.0 copy-start.4
  8.9 106.9 %all-gather.3.cloned.1.call-done = bf16[32,512,512]{2,1,0:T(8,128)(2,1)} async-done(((bf16[32,128,512]{2,1,0:T(8,128)(2,1)}), bf16[32,512,512]{2,1,0:T(8,128)(2,1)}) %all-gather.3.cloned.1.call-update) | async-done | bytes 16777232 | tf_op jit(solution)/shard_map/all_gather | solution.py:57
  115.8 26.4 %convert_bitcast_fusion.1 = bf16[1,32,512,512]{3,2,1,0:T(8,128)(2,1)} fusion(bf16[32,512,512]{2,1,0:T(8,128)(2,1)} %bitcast.95, bf16[32,512,512]{2,1,0:T(8,128)(2,1)} %all-gather.3.cloned.1.call-done, pred[32,512]{1,0:T(8,128)(4,1)S(1)} %constant_dynamic-slice_fusion), kind=kOutput, calls=%fused_computation.23 | convolution fusion | flops 8615100416 | bytes 50348032 | tf_op jit(solution)/shard_map/ikj,ijd->ikd/dot_general | solution.py:68
  142.1 0.0 copy-done.4
  142.1 20.2 copy.82
  162.3 6.2 all-to-all-start.2
  168.6 0.3 reduce-window.9
  168.9 0.1 slice.7
  169.0 0.1 slice_reduce_fusion
  169.2 0.1 bitcast_subtract_fusion
  169.2 0.1 add_bitcast_fusion
  169.4 0.1 copy.75
  169.4 0.0 copy-start.2
  169.4 2.9 compare_select_fusion.9
  172.4 10.0 reshape.71
  182.4 364.9 %all-to-all-done.2 = bf16[1,32,512,512]{3,1,0,2:T(8,128)(2,1)} async-done(((bf16[1,32,512,512]{3,1,0,2:T(8,128)(2,1)}), bf16[1,32,512,512]{3,1,0,2:T(8,128)(2,1)}, u32[]{:S(2)}, u32[]{:S(2)}) %all-to-all-start.2) | async-done | bytes 16777248 | tf_op jit(solution)/shard_map/all_to_all | solution.py:20
  547.3 16.9 copy.83
  564.2 0.0 copy-done.2
  564.2 37.1 %fusion.6 = bf16[8,4,32,16,512]{4,2,0,1,3:T(8,128)(2,1)} fusion(bf16[8,4,32,16,512,1]{4,3,1,0,2,5:T(8,128)(2,1)} %bitcast.90, bf16[16,8,32,8,32,1]{4,3,2,1,0,5:T(8,128)(2,1)} %bitcast.88), kind=kOutput, calls=%fused_computation.15 | convolution fusion | flops 4303355904 | bytes 35651584 | tf_op jit(solution)/shard_map/kpqsi,scikd->pcqkd/dot_general | solution.py:76
  601.3 15.9 copy.87
  617.2 365.9 %all_to_all.54 = bf16[32,32,16,512]{3,2,1,0:T(8,128)(2,1)} all-to-all(bf16[32,32,16,512]{3,2,1,0:T(8,128)(2,1)S(1)} %bitcast.87), channel_id=1, replica_groups=mesh['seq'=8,'ch'=4] {'seq','ch'}, dimensions={0} | all-to-all | bytes 33554432 | tf_op jit(solution)/shard_map/all_to_all | solution.py:36
  983.2 9.9 convert_bitcast_fusion
  993.0 11.6 copy.88
  1004.6 0.0 all-gather.5.cloned.1.call-done
  1004.6 0.0 copy-done
  1004.6 63.6 %fusion.4 = (bf16[16384,512]{1,0:T(8,128)(2,1)}, bf16[16384,512]{1,0:T(8,128)(2,1)}, bf16[16384,512]{1,0:T(8,128)(2,1)}) fusion(f32[1,32,32,16,512]{4,3,2,1,0:T(8,128)} %copy.88, bf16[16384,512]{1,0:T(8,128)(2,1)} %param.8, bf16[16384,2048]{1,0:T(8,128)(2,1)} %all-gather.5.cloned.1.call-done, bf16[2048,512]{1,0:T(8,128)(2,1)S(1)} %copy-done), kind=kOutput, calls=%fused_computation.9 | convolution fusion | flops 34468790272 | bytes 169869312 | tf_op jit(solution)/shard_map/dot_general | solution.py:80
  1068.2 15.9 copy.72
  1084.1 367.1 %all_to_all.55 = bf16[1,32,512,512]{3,1,0,2:T(8,128)(2,1)S(1)} all-to-all(bf16[1,32,512,512]{3,1,0,2:T(8,128)(2,1)S(1)} %copy.72), channel_id=1, replica_groups=mesh['seq'=8,'ch'=4] {'seq','ch'}, dimensions={2} | all-to-all | bytes 33554432 | tf_op jit(solution)/shard_map/all_to_all | solution.py:20
  1451.2 20.5 copy.73
  1471.8 35.7 %fusion.5 = bf16[8,4,32,16,512]{4,2,0,1,3:T(8,128)(2,1)} fusion(bf16[8,4,32,16,512,1]{4,3,1,0,2,5:T(8,128)(2,1)} %bitcast.84, bf16[16,8,32,8,32,1]{4,3,2,1,0,5:T(8,128)(2,1)} %bitcast.89), kind=kOutput, calls=%fused_computation.14 | convolution fusion | flops 4303355904 | bytes 35651584 | tf_op jit(solution)/shard_map/kpqsi,pcqkd->scikd/dot_general | solution.py:100
  1507.4 18.5 copy.79
  1525.9 4.2 all-to-all-start.1
  1530.1 0.0 reduce-scatter.5.cloned.1.call-start
  1530.1 44.5 %fusion.31 = bf16[2048,512]{0,1:T(8,128)(2,1)} fusion(bf16[16384,512]{1,0:T(8,128)(2,1)} %get-tuple-element.30, bf16[16384,2048]{1,0:T(8,128)(2,1)} %all-gather.5.cloned.1.call-done), kind=kOutput, calls=%fused_computation.36 | convolution fusion | flops 34360786944 | bytes 85983232 | tf_op jit(solution)/shard_map/te,tc->ec/dot_general | solution.py:85
  1574.6 0.0 reduce-scatter.5.cloned.1.call-update
  1574.6 0.0 reduce-scatter.3.cloned.1.call-start
  1574.6 350.6 %all-to-all-done.1 = bf16[32,32,16,512]{3,2,1,0:T(8,128)(2,1)} async-done(((bf16[32,32,16,512]{3,2,1,0:T(8,128)(2,1)}), bf16[32,32,16,512]{3,2,1,0:T(8,128)(2,1)}, u32[]{:S(2)}, u32[]{:S(2)}) %all-to-all-start.1) | async-done | bytes 16777248 | tf_op jit(solution)/shard_map/all_to_all | solution.py:36
  1925.3 0.0 copy-start.5
  1925.3 14.1 copy.80
  1939.4 0.0 copy-done.5
  1939.4 21.5 %fusion = bf16[32,512,512]{2,1,0:T(8,128)(2,1)} fusion(pred[32,512]{1,0:T(8,128)(4,1)S(1)} %copy-done.5, bf16[32,512,512]{2,1,0:T(8,128)(2,1)} %bitcast.92, bf16[32,512,512]{2,1,0:T(8,128)(2,1)} %bitcast.96), kind=kOutput, calls=%fused_computation.2 | convolution fusion | flops 8615100416 | bytes 50348032 | tf_op jit(solution)/shard_map/ikd,ijd->ikj/dot_general | solution.py:105
  1960.9 0.0 reduce-scatter.3.cloned.1.call-update
  1960.9 0.0 reduce-scatter.5.cloned.1.call-done
  1961.0 1.8 copy.92
  1962.8 85.1 %fusion.21 = bf16[16,8,32,8,32]{4,2,3,1,0:T(8,128)(2,1)} fusion(bf16[8,4,32,16,512,1]{4,3,1,0,2,5:T(8,128)(2,1)} %bitcast.91, bf16[8,4,32,16,512,1]{4,3,1,0,2,5:T(8,128)(2,1)} %bitcast.85), kind=kOutput, calls=%fused_computation.27 | convolution fusion | flops 4294967296 | bytes 35651584 | tf_op jit(solution)/shard_map/pcqkd,scikd->kpqsi/dot_general | solution.py:97
  2047.9 0.0 copy-start.3
  2047.9 15.5 copy.91
  2063.4 9.8 reshape.79
  2073.2 0.0 copy-done.3
  2073.2 1.7 fusion.30
  2074.9 0.0 copy-start.1
  2074.9 23.9 %fusion.16 = bf16[32,512,512]{2,1,0:T(8,128)(2,1)} fusion(bf16[32,512,512]{2,1,0:T(8,128)(2,1)} %bitcast.93, bf16[32,512,512]{2,1,0:T(8,128)(2,1)} %all-gather.3.cloned.1.call-done, pred[32,512]{1,0:T(8,128)(4,1)S(1)} %copy-done.5), kind=kOutput, calls=%fused_computation.26 | convolution fusion | flops 8615100416 | bytes 50348032 | tf_op jit(solution)/shard_map/ikj,ikd->ijd/dot_general | solution.py:112
  2098.8 0.0 reduce-scatter.3.cloned.1.call-done
  2098.8 0.0 copy-done.1
  (3 shorter events, 0.1 us)
Async XLA Ops:
  7.2 997.5 %copy-start = (bf16[2048,512]{1,0:T(8,128)(2,1)S(1)}, bf16[2048,512]{1,0:T(8,128)(2,1)}, u32[]{:S(2)}) copy-start(bf16[2048,512]{1,0:T(8,128)(2,1)} %param.12) | copy-start | bytes 6291460
  7.2 1.5 copy-start.6
  7.2 108.6 %all-gather.3.cloned.1.call-start = ((), (), s32[]{:S(2)}) async-start(), calls=%async_computation.6 | async-start | bytes 20971520 | tf_op jit(solution)/shard_map/all_gather | solution.py:57
  7.9 996.7 %all-gather.5.cloned.1.call-start = ((), (), s32[]{:S(2)}) async-start(), calls=%async_computation.7 | async-start | bytes 83886080 | tf_op jit(solution)/shard_map/all_gather | solution.py:56
  8.9 133.3 %copy-start.4 = (pred[32,512]{1,0:T(8,128)(4,1)}, pred[32,512]{1,0:T(8,128)(4,1)S(1)}, u32[]{:S(2)}) copy-start(pred[32,512]{1,0:T(8,128)(4,1)S(1)} %constant_dynamic-slice_fusion) | copy-start | bytes 49156
  162.3 385.0 %all-to-all-start.2 = ((bf16[1,32,512,512]{3,1,0,2:T(8,128)(2,1)}), bf16[1,32,512,512]{3,1,0,2:T(8,128)(2,1)}, u32[]{:S(2)}, u32[]{:S(2)}) async-start(bf16[1,32,512,512]{3,1,0,2:T(8,128)(2,1)} %copy.82), calls=%async_computation.2 | async-start | bytes 33554432 | tf_op jit(solution)/shard_map/all_to_all | solution.py:20
  169.4 394.8 %copy-start.2 = (s32[16,256]{1,0:T(8,128)}, s32[16,256]{1,0:T(8,128)S(1)}, u32[]{:S(2)}) copy-start(s32[16,256]{1,0:T(8,128)S(1)} %copy.75) | copy-start | bytes 49156
  1525.9 399.4 %all-to-all-start.1 = ((bf16[32,32,16,512]{3,2,1,0:T(8,128)(2,1)}), bf16[32,32,16,512]{3,2,1,0:T(8,128)(2,1)}, u32[]{:S(2)}, u32[]{:S(2)}) async-start(bf16[32,32,16,512]{3,2,1,0:T(8,128)(2,1)} %bitcast.86), calls=%async_computation.1 | async-start | bytes 33554432 | tf_op jit(solution)/shard_map/all_to_all | solution.py:36
  1530.1 430.9 %reduce-scatter.5.cloned.1.call-start = ((), (), s32[]{:S(2)}) async-start(), calls=%async_computation.9 | async-start | bytes 2359296 | tf_op jit(solution)/shard_map/reduce_scatter | solution.py:84
  1574.6 524.2 %reduce-scatter.3.cloned.1.call-start = ((), (), s32[]{:S(2)}) async-start(), calls=%async_computation.8 | async-start | bytes 20971520 | tf_op jit(solution)/shard_map/reduce_scatter | solution.py:109
  1925.3 14.1 copy-start.5
  2047.9 25.3 %copy-start.3 = (s32[16,256]{1,0:T(8,128)S(1)}, s32[16,256]{1,0:T(8,128)}, u32[]{:S(2)}) copy-start(s32[16,256]{1,0:T(8,128)} %copy-done.2) | copy-start | bytes 49156
  2074.9 23.9 %copy-start.1 = (bf16[2048,512]{1,0:T(8,128)(2,1)S(1)}, bf16[2048,512]{1,0:T(8,128)(2,1)}, u32[]{:S(2)}) copy-start(bf16[2048,512]{1,0:T(8,128)(2,1)} %param.12) | copy-start | bytes 6291460
Sparse Core Ops, SparseCore 0:
  9.6 106.1 all-gather.2
  117.3 712.8 all-gather.4
  1574.7 177.2 reduce-scatter.4
  1961.1 122.2 reduce-scatter.2
where the time goes:
time: 2110 us
  waiting for transfers between devices  824 us (39%)
  blocking collectives  733 us (35%)
  matrix products  338 us (16%)
  local copies, waits for them, and re-layouts  171 us (8%)
    all_to_all x1, blocking collectives, to_offsets(): lax.all_to_all(blocked.reshape(1, block_count, block_span, channels), ('s...  367 us
    all_to_all x1, blocking collectives, to_blocks(): lax.all_to_all(spread.reshape(seq_count * ch_count, block_count, offsets,...  366 us
    all_to_all x1, waiting for transfers between devices, to_offsets(): lax.all_to_all(blocked.reshape(1, block_count, block_span, channels), ('s...  365 us
    all_to_all x1, waiting for transfers between devices, to_blocks(): lax.all_to_all(spread.reshape(seq_count * ch_count, block_count, offsets,...  351 us
    all_gather x1, waiting for transfers between devices, on_device(): lax.all_gather(block_weight, 'ch', axis=1, tiled=True)  107 us
    dot_general x1, matrix products, on_device(): jnp.einsum('pcqkd,scikd->kpqsi', grad_spread, section_spread, preferred_e...  85.1 us
    dot_general x1, matrix products, on_device(): jnp.dot(full_grad, out_weight, preferred_element_type=jnp.float32)  63.6 us
    dot_general x1, matrix products, on_device(): jnp.einsum('te,tc->ec', full_grad, gated_out, preferred_element_type=jnp....  44.5 us
  transfers between devices with their start and end apart: 6, of which 3 were waited for; matrix products, arithmetic and copies ran while one was open for 18% of the time, Pallas kernels for 0%

commit v1 on v0

v1 whole, which is shorter than its diff:
```python
import jax
import jax.numpy as jnp
from jax import lax
from jax.sharding import PartitionSpec as P


IN_ONE = (2, 4, 10)
IN_TWO = (8, 8)
OUT_ONE = (16,)
OUT_TWO = (9, 5, 2)


def side_flags_of(reset_offset, block_span):
    within = jnp.arange(block_span, dtype=jnp.int32)
    return within[None, :] >= reset_offset[:, None]


def document_ids(reset_offset, block_span):
    starts = (reset_offset < block_span).astype(jnp.int32)
    earlier = jnp.cumsum(starts) - starts
    return earlier[:, None] + side_flags_of(reset_offset, block_span).astype(jnp.int32)


def spans_of(shares, block_count):
    cuts = [0]
    for share in shares:
        cuts.append(cuts[-1] + share)
    cuts = [cut * block_count // 16 for cut in cuts]
    return list(zip(cuts, cuts[1:]))


def scatter_sum(part, axis_name, dim):
    count = lax.axis_size(axis_name)
    index = lax.axis_index(axis_name)
    shape = part.shape
    part = part.reshape(*shape[:dim], count, shape[dim] // count, *shape[dim + 1 :])
    for n in range((count - 1).bit_length()):
        left = part.shape[dim] // 2
        part = part.reshape(*part.shape[:dim], left, 2, *part.shape[dim + 1 :])
        bit = (index >> n) & 1
        kept = lax.dynamic_index_in_dim(part, bit, dim + 1, keepdims=False)
        sent = lax.dynamic_index_in_dim(part, 1 - bit, dim + 1, keepdims=False)
        came = lax.ppermute(sent, axis_name, [(i, i ^ (1 << n)) for i in range(count)])
        part = (kept.astype(jnp.float32) + came.astype(jnp.float32)).astype(part.dtype)
    return part.reshape(*shape[:dim], shape[dim] // count, *shape[dim + 1 :])


def to_offsets(blocked, seq_count):
    count, block_span, channels = blocked.shape
    places = block_span // seq_count
    split = blocked.reshape(count, seq_count, places, channels).transpose(1, 0, 2, 3)
    return lax.all_to_all(split, "seq", split_axis=0, concat_axis=0, tiled=True)


def to_blocks(spread, seq_count):
    arrived = lax.all_to_all(spread, "seq", split_axis=0, concat_axis=0, tiled=True)
    count, places, channels = arrived.shape[1:]
    return arrived.transpose(1, 0, 2, 3).reshape(count, seq_count * places, channels)


def on_device(
    block_input, gate_pre, out_grad, block_weight, offset_weight, out_weight, reset_offset
):
    seq_count = lax.axis_size("seq")
    token_count, channels = block_input.shape
    block_span = block_weight.shape[2]
    block_count = token_count // block_span
    places = block_span // seq_count
    seq_index = lax.axis_index("seq")
    side_table = side_flags_of(reset_offset, block_span)
    doc_table = document_ids(reset_offset, block_span)
    total_blocks = doc_table.shape[0]
    local_sides = lax.dynamic_slice_in_dim(side_table, seq_index * block_count, block_count, 0)
    inputs = block_input.reshape(block_count, block_span, channels)
    gates = gate_pre.reshape(block_count, block_span, channels)
    grads = out_grad.reshape(block_count, block_span, channels)

    def mask_one(lo, hi):
        sides = local_sides[lo:hi]
        return sides[:, :, None] == sides[:, None, :]

    weights, section_parts = [], []
    for lo, hi in spans_of(IN_ONE, block_count):
        gathered = lax.all_gather(block_weight[lo:hi], "ch", axis=1, tiled=True)
        masked = jnp.where(mask_one(lo, hi), gathered, jnp.zeros_like(gathered))
        weights.append(gathered)
        section = jnp.einsum(
            "ikj,ijd->ikd", masked, inputs[lo:hi], preferred_element_type=jnp.float32
        ).astype(jnp.bfloat16)
        section_parts.append(to_offsets(section, seq_count))
    full_weight = jnp.concatenate(weights, axis=0)
    section_spread = jnp.concatenate(section_parts, axis=1)

    full_grads, mixer_grads, grad_parts = [], [], []
    for lo, hi in spans_of(IN_TWO, block_count):
        gathered = lax.all_gather(grads[lo:hi], "ch", axis=2, tiled=True)
        full_grads.append(gathered)
        head_grad = jnp.dot(
            gathered.reshape(-1, out_weight.shape[0]),
            out_weight,
            preferred_element_type=jnp.float32,
        ).reshape(hi - lo, block_span, channels)
        sigmoid_gate = jax.nn.sigmoid(gates[lo:hi].astype(jnp.float32))
        mixer_grad = (head_grad * sigmoid_gate).astype(jnp.bfloat16)
        mixer_grads.append(mixer_grad)
        grad_parts.append(to_offsets(mixer_grad, seq_count))
    grad_spread = jnp.concatenate(grad_parts, axis=1)

    own_offsets = lax.all_gather(offset_weight, "ch", axis=0, tiled=True)
    labels = lax.dynamic_slice_in_dim(doc_table, seq_index * places, places, 1).T
    mask_two = labels[:, :, None] == labels[:, None, :]
    masked_two = jnp.where(mask_two, own_offsets, jnp.zeros_like(own_offsets))
    section_spread = section_spread.reshape(total_blocks, places, channels)
    grad_spread = grad_spread.reshape(total_blocks, places, channels)
    mixer_spread = jnp.einsum(
        "kmi,ikd->mkd", masked_two, section_spread, preferred_element_type=jnp.float32
    ).astype(jnp.bfloat16)
    mixer_spread = mixer_spread.reshape(seq_count, block_count, places, channels)
    mixer_parts = []
    for lo, hi in spans_of(OUT_ONE, block_count):
        mixer_parts.append(to_blocks(mixer_spread[:, lo:hi], seq_count))
    mixer_out = jnp.concatenate(mixer_parts)
    section_grad_spread = jnp.einsum(
        "kmi,mkd->ikd", masked_two, grad_spread, preferred_element_type=jnp.float32
    ).astype(jnp.bfloat16)
    section_grad_spread = section_grad_spread.reshape(seq_count, block_count, places, channels)
    offset_grad = jnp.einsum(
        "mkd,ikd->kmi", grad_spread, section_spread, preferred_element_type=jnp.float32
    )
    offset_grad = jnp.where(mask_two, offset_grad, jnp.zeros_like(offset_grad)).astype(jnp.bfloat16)
    offset_grad = lax.psum_scatter(offset_grad, "ch", scatter_dimension=0, tiled=True)

    full_grad = jnp.concatenate(full_grads, axis=0).reshape(token_count, -1)
    mixer_grad = jnp.concatenate(mixer_grads, axis=0)
    later_gates, mixer_out = lax.optimization_barrier((gates, mixer_out))
    sigmoid_gate = jax.nn.sigmoid(later_gates.astype(jnp.float32))
    mixer_float = mixer_out.astype(jnp.float32)
    gated_out = (mixer_float * sigmoid_gate).astype(jnp.bfloat16)
    gate_grad = (mixer_grad.astype(jnp.float32) * mixer_float * (1.0 - sigmoid_gate)).astype(
        jnp.bfloat16
    )
    weight_part = jnp.einsum(
        "te,tc->ec",
        full_grad,
        gated_out.reshape(token_count, channels),
        preferred_element_type=jnp.float32,
    ).astype(jnp.bfloat16)
    weight_share = scatter_sum(weight_part, "seq", 0)

    block_grad = jnp.zeros(block_weight.shape, jnp.bfloat16)
    input_grad = jnp.zeros(inputs.shape, jnp.bfloat16)
    for n, (lo, hi) in enumerate(spans_of(OUT_TWO, block_count)):
        section_grad = to_blocks(section_grad_spread[:, lo:hi], seq_count)
        mask = mask_one(lo, hi)
        partial_grad = jnp.einsum(
            "ikd,ijd->ikj", section_grad, inputs[lo:hi], preferred_element_type=jnp.float32
        )
        partial_grad = jnp.where(mask, partial_grad, jnp.zeros_like(partial_grad))
        partial_grad = partial_grad.astype(jnp.bfloat16)
        if n == len(OUT_TWO) - 1:
            reduced = scatter_sum(partial_grad, "ch", 1)
        else:
            reduced = lax.psum_scatter(partial_grad, "ch", scatter_dimension=1, tiled=True)
        block_grad = lax.dynamic_update_slice(block_grad, reduced, (lo, 0, 0))
        weight = full_weight[lo:hi]
        masked = jnp.where(mask, weight, jnp.zeros_like(weight))
        returned = jnp.einsum(
            "ikj,ikd->ijd", masked, section_grad, preferred_element_type=jnp.float32
        ).astype(jnp.bfloat16)
        input_grad = lax.dynamic_update_slice(input_grad, returned, (lo, 0, 0))
    return (
        input_grad.reshape(token_count, channels),
        gate_grad.reshape(token_count, channels),
        block_grad,
        offset_grad,
        weight_share,
    )


def solution(mesh):
    in_specs = (
        P("seq", "ch"),
        P("seq", "ch"),
        P("seq", "ch"),
        P("seq", "ch", None),
        P(("seq", "ch"), None, None),
        P(None, "ch"),
        P(),
    )
    out_specs = (
        P("seq", "ch"),
        P("seq", "ch"),
        P("seq", "ch", None),
        P(("seq", "ch"), None, None),
        P("seq", "ch"),
    )
    return jax.shard_map(
        on_device, mesh=mesh, in_specs=in_specs, out_specs=out_specs, check_vma=False
    )
```

time: 2110 us -> 1850 us (0.88)
  blocking collectives: 733 us -> 0 us
  waiting for transfers between devices: 824 us -> 1250 us
  matrix products: 338 us -> 223 us
  local copies, waits for them, and re-layouts: 171 us -> 235 us
  other arithmetic: 15.2 us -> 68.2 us
  starting transfers between devices: 10.6 us -> 57.6 us
    all_to_all x2 -> x0, blocking collectives: 733 us -> none  [the longest x1 367 us: to_offsets(): lax.all_to_all(blocked.reshape(1, block_count, block_span, channels), ('s...]
    all_gather x2 -> x6, waiting for transfers between devices: 107 us -> 382 us  [the longest x2 309 us: on_device(): gathered = lax.all_gather(grads[lo:hi], 'ch', axis=2, tiled=True)]
    dot_general x8 -> x15, matrix products: 338 us -> 223 us  [the longest x2 59.7 us: on_device(): jnp.dot(gathered.reshape(-1, out_weight.shape[0]), out_weight, preferred_...]
    all_to_all x2 -> x9, waiting for transfers between devices: 716 us -> 827 us  [the longest x4 558 us: to_blocks(): lax.all_to_all(spread, 'seq', split_axis=0, concat_axis=0, tiled=True)]
    slice x1 -> x19, local copies, waits for them, and re-layouts: 0.07 us -> 74.7 us  [the longest x6 28.7 us: on_device(): inputs[lo:hi]]
    all_to_all x3 -> x0, local copies, waits for them, and re-layouts: 51.5 us -> none  [the longest x2 37.4 us: to_offsets(): lax.all_to_all(blocked.reshape(1, block_count, block_span, channels), ('s...]
    convert_element_type x3 -> x0, local copies, waits for them, and re-layouts: 46 us -> none  [the longest x1 18.5 us: on_device(): section_grad_spread = jnp.einsum('kpqsi,pcqkd->scikd', masked_two, grad_s...]
    concatenate x0 -> x2, local copies, waits for them, and re-layouts: none -> 42.5 us  [the longest x1 21.2 us: on_device(): grad_spread = jnp.concatenate(grad_parts, axis=1)]
  transfers between devices with their start and end apart: 6 -> 23, of which waited for: 3 -> 14; matrix products, arithmetic and copies ran while one was open for 18% -> 28% of each run, Pallas kernels for 0% -> 0%
where the time goes in v1:
time: 1850 us
  waiting for transfers between devices  1250 us (68%)
  local copies, waits for them, and re-layouts  235 us (13%)
  matrix products  223 us (12%)
  other arithmetic  68.2 us (4%)
  starting transfers between devices  57.6 us (3%)
    all_to_all x4, waiting for transfers between devices, to_blocks(): lax.all_to_all(spread, 'seq', split_axis=0, concat_axis=0, tiled=True)  558 us
    all_gather x2, waiting for transfers between devices, on_device(): gathered = lax.all_gather(grads[lo:hi], 'ch', axis=2, tiled=True)  309 us
    all_to_all x5, waiting for transfers between devices, to_offsets(): return lax.all_to_all(split, 'seq', split_axis=0, concat_axis=0, tiled=True)  270 us
    dot_general x2, matrix products, on_device(): jnp.dot(gathered.reshape(-1, out_weight.shape[0]), out_weight, preferred_...  59.7 us
    dot_general x1, matrix products, on_device(): jnp.einsum('te,tc->ec', full_grad, gated_out.reshape(token_count, channel...  46.2 us
    all_gather x3, waiting for transfers between devices, on_device(): gathered = lax.all_gather(block_weight[lo:hi], 'ch', axis=1, tiled=True)  43.1 us
  transfers between devices with their start and end apart: 23, of which 14 were waited for; matrix products, arithmetic and copies ran while one was open for 28% of the time, Pallas kernels for 0%

profile of v1, /device:TPU:6, one launch (start us, length us, event | category | flops | bytes accessed | tf_op | source)
XLA Modules:
  0.0 1845.4 jit_solution(4656502029321814694)
XLA Ops:
  11.7 11.9 fusion.70
  25.0 4.5 fusion.69
  29.5 3.5 all-gather.7.cloned.1.call-done
  33.0 3.5 fusion.50
  38.0 6.1 all-to-all-start.5
  44.1 5.2 slice.132
  49.3 20.4 %all-gather.9.cloned.1.call-done = bf16[8,512,512]{2,1,0:T(8,128)(2,1)} async-done(((bf16[8,128,512]{2,1,0:T(8,128)(2,1)}), bf16[8,512,512]{2,1,0:T(8,128)(2,1)}) %all-gather.9.cloned.1.call-update) | async-done | bytes 4194320 | tf_op jit(solution)/shard_map/all_gather | solution.py:84
  69.6 5.5 fusion.36
  77.6 14.6 all-to-all-done.5
  92.2 5.4 all-to-all-start.6
  97.7 19.9 %add_divide_fusion.2 = (f32[8192,512]{1,0:T(8,128)}, f32[8192,512]{1,0:T(8,128)}) fusion(bf16[16384,512]{1,0:T(8,128)(2,1)} %param.8), kind=kLoop, calls=%fused_computation.22 | loop fusion | flops 33554432 | bytes 50331648 | tf_op jit(solution)/shard_map/div | solution.py:103
  117.6 155.1 %all-gather.13.cloned.1.call-done = bf16[16,512,2048]{2,1,0:T(8,128)(2,1)} async-done(((bf16[16,512,512]{2,1,0:T(8,128)(2,1)}), bf16[16,512,2048]{2,1,0:T(8,128)(2,1)}) %all-gather.13.cloned.1.call-update) | async-done | bytes 33554448 | tf_op jit(solution)/shard_map/all_gather | solution.py:96
  272.7 30.6 %multiply_convert_fusion.1 = bf16[16,512,512]{2,1,0:T(8,128)(2,1)} fusion(f32[16,512,512]{2,1,0:T(8,128)} %bitcast.130, bf16[16,512,2048]{2,1,0:T(8,128)(2,1)} %all-gather.13.cloned.1.call-done, bf16[2048,512]{1,0:T(8,128)(2,1)S(1)} %copy-done), kind=kOutput, calls=%fused_computation.21 | convolution fusion | flops 17188257792 | bytes 60817408 | tf_op jit(solution)/shard_map/dot_general | solution.py:98
  303.3 8.3 copy.87
  311.6 6.0 all-to-all-start
  318.2 3.5 slice.111
  321.7 154.0 %all-gather.15.cloned.1.call-done = bf16[16,512,2048]{2,1,0:T(8,128)(2,1)} async-done(((bf16[16,512,512]{2,1,0:T(8,128)(2,1)}), bf16[16,512,2048]{2,1,0:T(8,128)(2,1)}) %all-gather.15.cloned.1.call-update) | async-done | bytes 33554448 | tf_op jit(solution)/shard_map/all_gather | solution.py:96
  475.7 29.1 %multiply_convert_fusion = bf16[16,512,512]{2,1,0:T(8,128)(2,1)} fusion(f32[16,512,512]{2,1,0:T(8,128)} %bitcast.129, bf16[16,512,2048]{2,1,0:T(8,128)(2,1)} %all-gather.15.cloned.1.call-done, bf16[2048,512]{1,0:T(8,128)(2,1)S(1)} %copy-done), kind=kOutput, calls=%fused_computation.19 | convolution fusion | flops 17188257792 | bytes 60817408 | tf_op jit(solution)/shard_map/dot_general | solution.py:98
  504.8 7.8 copy.86
  512.7 6.1 all-to-all-start.1
  518.7 9.9 slice.135
  528.6 19.3 %all-gather.11.cloned.1.call-done = bf16[20,512,512]{2,1,0:T(8,128)(2,1)} async-done(((bf16[20,128,512]{2,1,0:T(8,128)(2,1)}), bf16[20,512,512]{2,1,0:T(8,128)(2,1)}) %all-gather.11.cloned.1.call-update) | async-done | bytes 10485776 | tf_op jit(solution)/shard_map/all_gather | solution.py:84
  547.9 13.8 fusion.19
  561.7 9.6 copy.85
  571.3 130.3 %all-to-all-done.1 = bf16[8,16,64,512]{3,2,1,0:T(8,128)(2,1)} async-done(((bf16[8,16,64,512]{3,2,1,0:T(8,128)(2,1)}), bf16[8,16,64,512]{3,2,1,0:T(8,128)(2,1)}, u32[]{:S(2)}, u32[]{:S(2)}) %all-to-all-start.1) | async-done | bytes 8388640 | tf_op jit(solution)/shard_map/all_to_all | solution.py:52
  701.7 5.7 all-to-all-start.7
  708.8 8.0 pad_maximum_fusion
  716.8 21.2 %copy.43 = bf16[8,32,64,512]{3,1,0,2:T(8,128)(2,1)} copy(bf16[8,32,64,512]{3,2,1,0:T(8,128)(2,1)S(1)} %pad_maximum_fusion) | data formatting | bytes 33554432 | tf_op jit(solution)/shard_map/concatenate | solution.py:107
  738.0 29.6 %all-gather.17.cloned.1.call-done = bf16[64,256,256]{2,1,0:T(8,128)(2,1)} async-done(((bf16[16,256,256]{2,1,0:T(8,128)(2,1)}), bf16[64,256,256]{2,1,0:T(8,128)(2,1)}) %all-gather.17.cloned.1.call-update) | async-done | bytes 8388624 | tf_op jit(solution)/shard_map/all_gather | solution.py:109
  767.7 17.9 convolution_convert_fusion.1
  785.6 10.7 slice.143
  796.3 13.4 copy.71
  809.7 124.7 %all-to-all-done.7 = bf16[8,20,64,512]{3,2,1,0:T(8,128)(2,1)} async-done(((bf16[8,20,64,512]{3,2,1,0:T(8,128)(2,1)}), bf16[8,20,64,512]{3,2,1,0:T(8,128)(2,1)}, u32[]{:S(2)}, u32[]{:S(2)}) %all-to-all-start.7) | async-done | bytes 10485792 | tf_op jit(solution)/shard_map/all_to_all | solution.py:52
  934.5 5.7 all-to-all-start.2
  940.2 11.4 slice.145
  951.7 8.8 copy.72
  960.5 183.7 %all-to-all-done.2 = bf16[8,18,64,512]{3,2,1,0:T(8,128)(2,1)} async-done(((bf16[8,18,64,512]{3,2,1,0:T(8,128)(2,1)}), bf16[8,18,64,512]{3,2,1,0:T(8,128)(2,1)}, u32[]{:S(2)}, u32[]{:S(2)}) %all-to-all-start.2) | async-done | bytes 9437216 | tf_op jit(solution)/shard_map/all_to_all | solution.py:56
  1144.1 5.6 all-to-all-start.3
  1149.7 9.1 slice.137
  1158.8 8.0 pad_maximum_fusion.1
  1166.9 21.2 %copy.59 = bf16[8,32,64,512]{3,1,0,2:T(8,128)(2,1)} copy(bf16[8,32,64,512]{3,2,1,0:T(8,128)(2,1)S(1)} %pad_maximum_fusion.1) | data formatting | bytes 33554432 | tf_op jit(solution)/shard_map/concatenate | solution.py:92
  1188.1 13.2 convolution_convert_fusion
  1201.3 18.5 %copy.60 = bf16[8,32,64,512]{3,2,1,0:T(8,128)(2,1)} copy(bf16[8,32,64,512]{3,1,0,2:T(8,128)(2,1)} %bitcast.113) | data formatting | bytes 33554432 | tf_op jit(solution)/shard_map/reshape | solution.py:118
  1219.8 8.6 copy.48
  1228.4 35.9 %all-to-all-done.3 = bf16[8,10,64,512]{3,2,1,0:T(8,128)(2,1)} async-done(((bf16[8,10,64,512]{3,2,1,0:T(8,128)(2,1)}), bf16[8,10,64,512]{3,2,1,0:T(8,128)(2,1)}, u32[]{:S(2)}, u32[]{:S(2)}) %all-to-all-start.3) | async-done | bytes 5242912 | tf_op jit(solution)/shard_map/all_to_all | solution.py:56
  1264.3 6.2 all-to-all-start.8
  1270.5 12.6 fusion.7
  1283.3 3.0 copy.51
  1288.5 4.9 fusion.10
  1293.4 338.2 %all-to-all-done.8 = bf16[8,32,64,512]{3,2,1,0:T(8,128)(2,1)} async-done(((bf16[8,32,64,512]{3,2,1,0:T(8,128)(2,1)}), bf16[8,32,64,512]{3,2,1,0:T(8,128)(2,1)}, u32[]{:S(2)}, u32[]{:S(2)}) %all-to-all-start.8) | async-done | bytes 16777248 | tf_op jit(solution)/shard_map/all_to_all | solution.py:56
  1631.6 14.0 copy.61
  1645.6 3.5 slice.147
  1651.2 4.6 all-to-all-start.4
  1656.0 15.5 fusion.8
  1671.5 46.2 %bitcast_convert_fusion = bf16[2048,512]{1,0:T(8,128)(2,1)S(1)} fusion(bf16[32,512,512]{2,1,0:T(8,128)(2,1)} %bitcast.117, bf16[32,512,512]{2,1,0:T(8,128)(2,1)} %bitcast.115, bf16[16,512,2048]{2,1,0:T(8,128)(2,1)} %all-gather.15.cloned.1.call-done, bf16[16,512,2048]{2,1,0:T(8,128)(2,1)} %all-gather.13.cloned.1.call-done), kind=kOutput, calls=%fused_computation.54 | convolution fusion | flops 34453061632 | bytes 102760448 | tf_op jit(solution)/shard_map/te,tc->ec/dot_general | solution.py:142
  1719.4 24.6 %collective-permute-done.2 = bf16[4,256,512]{2,1,0:T(8,128)(2,1)} collective-permute-done((bf16[4,256,512]{2,1,0:T(8,128)(2,1)S(1)}, bf16[4,256,512]{2,1,0:T(8,128)(2,1)}, u32[]{:S(2)}, u32[]{:S(2)}) %collective-permute-start.2) | collective-permute-done | bytes 1048608 | tf_op jit(solution)/shard_map/ppermute | solution.py:43
  1748.1 11.5 collective-permute-done.3
  1764.5 3.9 fusion.26
  1768.8 25.5 %fusion.5 = bf16[32,512,512]{2,1,0:T(8,128)(2,1)} fusion(bf16[32,512,512]{2,1,0:T(8,128)(2,1)} %bitcast.118, bf16[16,512,512]{2,1,0:T(8,128)(2,1)} %multiply_convert_fusion, bf16[16,512,512]{2,1,0:T(8,128)(2,1)} %multiply_convert_fusion.1, bf16[32,512,512]{2,1,0:T(8,128)(2,1)} %bitcast.116), kind=kLoop, calls=%fused_computation.7 | loop fusion | flops 92274688 | bytes 67108864 | tf_op jit(solution)/shard_map/convert_element_type | solution.py:139
  1797.1 14.2 fusion.18
  1811.3 6.1 dynamic_update_slice.18
  1817.5 8.1 convert_dynamic-update-slice_fusion
  1825.5 4.5 convert_dynamic-update-slice_fusion.1
  1830.1 4.2 dynamic_update_slice.21
  (101 shorter events, 34.7 us)
Async XLA Ops:
  7.2 265.6 %copy-start = (bf16[2048,512]{1,0:T(8,128)(2,1)S(1)}, bf16[2048,512]{1,0:T(8,128)(2,1)}, u32[]{:S(2)}) copy-start(bf16[2048,512]{1,0:T(8,128)(2,1)} %param.12) | copy-start | bytes 6291460
  7.2 25.8 %all-gather.7.cloned.1.call-start = ((), (), s32[]{:S(2)}) async-start(), calls=%async_computation.12 | async-start | bytes 2621440 | tf_op jit(solution)/shard_map/all_gather | solution.py:84
  9.3 60.3 %all-gather.9.cloned.1.call-start = ((), (), s32[]{:S(2)}) async-start(), calls=%async_computation.13 | async-start | bytes 5242880 | tf_op jit(solution)/shard_map/all_gather | solution.py:84
  11.6 261.1 %all-gather.13.cloned.1.call-start = ((), (), s32[]{:S(2)}) async-start(), calls=%async_computation.15 | async-start | bytes 41943040 | tf_op jit(solution)/shard_map/all_gather | solution.py:96
  23.5 0.7 copy-start.10
  23.6 452.1 %all-gather.15.cloned.1.call-start = ((), (), s32[]{:S(2)}) async-start(), calls=%async_computation.16 | async-start | bytes 41943040 | tf_op jit(solution)/shard_map/all_gather | solution.py:96
  38.0 54.2 %all-to-all-start.5 = ((bf16[8,4,64,512]{3,2,1,0:T(8,128)(2,1)}), bf16[8,4,64,512]{3,2,1,0:T(8,128)(2,1)}, u32[]{:S(2)}, u32[]{:S(2)}) async-start(bf16[8,4,64,512]{3,2,1,0:T(8,128)(2,1)} %bitcast.143), calls=%async_computation.5 | async-start | bytes 4194304 | tf_op jit(solution)/shard_map/all_to_all | solution.py:52
  92.2 219.4 %all-to-all-start.6 = ((bf16[8,8,64,512]{3,2,1,0:T(8,128)(2,1)}), bf16[8,8,64,512]{3,2,1,0:T(8,128)(2,1)}, u32[]{:S(2)}, u32[]{:S(2)}) async-start(bf16[8,8,64,512]{3,2,1,0:T(8,128)(2,1)} %bitcast.133), calls=%async_computation.6 | async-start | bytes 8388608 | tf_op jit(solution)/shard_map/all_to_all | solution.py:52
  311.6 201.0 %all-to-all-start = ((bf16[8,16,64,512]{3,2,1,0:T(8,128)(2,1)}), bf16[8,16,64,512]{3,2,1,0:T(8,128)(2,1)}, u32[]{:S(2)}, u32[]{:S(2)}) async-start(bf16[8,16,64,512]{3,2,1,0:T(8,128)(2,1)} %bitcast.120), calls=%async_computation | async-start | bytes 16777216 | tf_op jit(solution)/shard_map/all_to_all | solution.py:52
  317.7 230.2 %all-gather.11.cloned.1.call-start = ((), (), s32[]{:S(2)}) async-start(), calls=%async_computation.14 | async-start | bytes 13107200 | tf_op jit(solution)/shard_map/all_gather | solution.py:84
  512.7 189.0 %all-to-all-start.1 = ((bf16[8,16,64,512]{3,2,1,0:T(8,128)(2,1)}), bf16[8,16,64,512]{3,2,1,0:T(8,128)(2,1)}, u32[]{:S(2)}, u32[]{:S(2)}) async-start(bf16[8,16,64,512]{3,2,1,0:T(8,128)(2,1)} %bitcast.121), calls=%async_computation.1 | async-start | bytes 16777216 | tf_op jit(solution)/shard_map/all_to_all | solution.py:52
  701.7 6.3 copy-start.11
  701.7 232.8 %all-to-all-start.7 = ((bf16[8,20,64,512]{3,2,1,0:T(8,128)(2,1)}), bf16[8,20,64,512]{3,2,1,0:T(8,128)(2,1)}, u32[]{:S(2)}, u32[]{:S(2)}) async-start(bf16[8,20,64,512]{3,2,1,0:T(8,128)(2,1)} %bitcast.119), calls=%async_computation.7 | async-start | bytes 20971520 | tf_op jit(solution)/shard_map/all_to_all | solution.py:52
  707.4 60.3 %all-gather.17.cloned.1.call-start = ((), (), s32[]{:S(2)}) async-start(), calls=%async_computation.17 | async-start | bytes 10485760 | tf_op jit(solution)/shard_map/all_gather | solution.py:109
  934.5 209.6 %all-to-all-start.2 = ((bf16[8,18,64,512]{3,2,1,0:T(8,128)(2,1)}), bf16[8,18,64,512]{3,2,1,0:T(8,128)(2,1)}, u32[]{:S(2)}, u32[]{:S(2)}) async-start(bf16[8,18,64,512]{3,2,1,0:T(8,128)(2,1)} %copy.71), calls=%async_computation.2 | async-start | bytes 18874368 | tf_op jit(solution)/shard_map/all_to_all | solution.py:56
  1144.1 120.2 %all-to-all-start.3 = ((bf16[8,10,64,512]{3,2,1,0:T(8,128)(2,1)}), bf16[8,10,64,512]{3,2,1,0:T(8,128)(2,1)}, u32[]{:S(2)}, u32[]{:S(2)}) async-start(bf16[8,10,64,512]{3,2,1,0:T(8,128)(2,1)} %copy.72), calls=%async_computation.3 | async-start | bytes 10485760 | tf_op jit(solution)/shard_map/all_to_all | solution.py:56
  1158.8 111.7 %copy-start.8 = (pred[18,512]{1,0:T(8,128)(4,1)}, pred[18,512]{1,0:T(8,128)(4,1)S(1)}, u32[]{:S(2)}) copy-start(pred[18,512]{1,0:T(8,128)(4,1)S(1)} %constant_dynamic-slice_fusion.3) | copy-start | bytes 27652
  1158.8 29.3 %slice-start.1 = ((s8[8388608]{0:T(1024)(128)(4,1)}), s8[4194304]{0:T(1024)(128)(4,1)S(1)}, s32[]{:S(2)}) async-start(s8[8388608]{0:T(1024)(128)(4,1)} %bitcast.135), calls=%async_computation.22 | async-start | bytes 8388608
  1166.9 21.2 %slice-start.2 = ((s8[8388608]{0:T(1024)(128)(4,1)}), s8[4194304]{0:T(1024)(128)(4,1)S(1)}, s32[]{:S(2)}) async-start(s8[8388608]{0:T(1024)(128)(4,1)} %bitcast.135), calls=%async_computation.23 | async-start | bytes 8388608
  1264.3 367.3 %all-to-all-start.8 = ((bf16[8,32,64,512]{3,2,1,0:T(8,128)(2,1)}), bf16[8,32,64,512]{3,2,1,0:T(8,128)(2,1)}, u32[]{:S(2)}, u32[]{:S(2)}) async-start(bf16[8,32,64,512]{3,2,1,0:T(8,128)(2,1)} %copy.60), calls=%async_computation.8 | async-start | bytes 33554432 | tf_op jit(solution)/shard_map/all_to_all | solution.py:56
  1270.5 559.6 %reduce-scatter.4.cloned.1.call-start = ((), (), s32[]{:S(2)}) async-start(), calls=%async_computation.18 | async-start | bytes 11796480 | tf_op jit(solution)/shard_map/reduce_scatter | solution.py:163
  1283.1 551.1 %reduce-scatter.6.cloned.1.call-start = ((), (), s32[]{:S(2)}) async-start(), calls=%async_computation.19 | async-start | bytes 6553600 | tf_op jit(solution)/shard_map/reduce_scatter | solution.py:163
  1283.2 5.3 slice-start
  1283.2 10.2 copy-start.12
  1286.3 2.2 copy-start.2
  1651.2 112.8 %all-to-all-start.4 = ((bf16[8,4,64,512]{3,1,2,0:T(4,128)(2,1)}), bf16[8,4,64,512]{3,1,2,0:T(4,128)(2,1)S(1)}, u32[]{:S(2)}, u32[]{:S(2)}) async-start(bf16[8,4,64,512]{3,1,2,0:T(4,128)(2,1)} %copy.73), calls=%async_computation.4 | async-start | bytes 4194304 | tf_op jit(solution)/shard_map/all_to_all | solution.py:56
  1655.8 182.8 %reduce-scatter.8.cloned.1.call-start = ((), (), s32[]{:S(2)}) async-start(), calls=%async_computation.20 | async-start | bytes 10485760 | tf_op jit(solution)/shard_map/reduce_scatter | solution.py:131
  1717.7 1.3 copy-start.3
  1717.7 46.8 %copy-start.14 = (pred[4,512]{1,0:T(4,128)(4,1)S(1)}, pred[4,512]{1,0:T(4,128)(4,1)}, u32[]{:S(2)}) copy-start(pred[4,512]{1,0:T(4,128)(4,1)} %get-tuple-element.18) | copy-start | bytes 6148
  1719.1 24.9 %collective-permute-start.2 = (bf16[4,256,512]{2,1,0:T(8,128)(2,1)S(1)}, bf16[4,256,512]{2,1,0:T(8,128)(2,1)}, u32[]{:S(2)}, u32[]{:S(2)}) collective-permute-start(bf16[4,256,512]{2,1,0:T(8,128)(2,1)S(1)} %dynamic-slice_bitcast_fusion), channel_id=1, source_target_pairs={{0,4},{4,0},{8,12},{12,8},{16,20},{20,16},{24,28},{28,24},{1,5},{5... | collective-permute-start | bytes 3145736 | tf_op jit(solution)/shard_map/ppermute | solution.py:43
  1746.7 13.0 collective-permute-start.3
  1760.8 0.8 copy-start.6
  1761.6 32.6 %collective-permute-start.4 = (bf16[1,256,512]{2,1,0:T(8,128)(2,1)S(1)}, bf16[1,256,512]{2,1,0:T(8,128)(2,1)S(1)}, u32[]{:S(2)}, u32[]{:S(2)}) collective-permute-start(bf16[1,256,512]{2,1,0:T(8,128)(2,1)S(1)} %constant_dynamic-slice_fusion.4), channel_id=1, source_target_pairs={{0,16},{4,20},{8,24},{12,28},{16,0},{20,4},{24,8},{28,12},{1,17},{... | collective-permute-start | bytes 786440 | tf_op jit(solution)/shard_map/ppermute | solution.py:43
  1764.5 4.2 copy-start.4
  1768.7 25.6 %copy-start.7 = (bf16[2,256,512]{2,1,0:T(8,128)(2,1)S(1)}, bf16[2,256,512]{2,1,0:T(8,128)(2,1)}, u32[]{:S(2)}) copy-start(bf16[2,256,512]{2,1,0:T(8,128)(2,1)} %copy-done.6) | copy-start | bytes 1572868
  1768.7 28.4 %copy-start.9 = (pred[18,512]{1,0:T(8,128)(4,1)S(1)}, pred[18,512]{1,0:T(8,128)(4,1)}, u32[]{:S(2)}) copy-start(pred[18,512]{1,0:T(8,128)(4,1)} %copy-done.8) | copy-start | bytes 27652
  1768.7 26.3 %collective-permute-start = (bf16[4,2,128,512]{3,2,0,1:T(8,128)(2,1)S(1)}, bf16[4,2,128,512]{3,2,0,1:T(8,128)(2,1)S(1)}, u32[]{:S(2)}, u32[]{:S(2)}) collective-permute-start(bf16[4,2,128,512]{3,2,0,1:T(8,128)(2,1)S(1)} %bitcast.158), channel_id=1, source_target_pairs={{0,1},{1,0},{2,3},{3,2},{4,5},{5,4},{6,7},{7,6},{8,9},{9,8},{10,11... | collective-permute-start | bytes 3145736 | tf_op jit(solution)/shard_map/ppermute | solution.py:43
  1796.2 40.5 %collective-permute-start.1 = (bf16[4,1,128,512]{3,2,0,1:T(8,128)(2,1)}, bf16[4,1,128,512]{3,2,0,1:T(8,128)(2,1)}, u32[]{:S(2)}, u32[]{:S(2)}) collective-permute-start(bf16[4,1,128,512]{3,2,0,1:T(8,128)(2,1)} %constant_dynamic-slice_fusion.5), channel_id=1, source_target_pairs={{0,2},{1,3},{2,0},{3,1},{4,6},{5,7},{6,4},{7,5},{8,10},{9,11},{10,... | collective-permute-start | bytes 1572872 | tf_op jit(solution)/shard_map/ppermute | solution.py:43
  1811.3 6.2 copy-start.13
  1817.5 8.1 copy-start.5
  1817.5 21.2 %copy-start.1 = (bf16[2048,512]{1,0:T(8,128)(2,1)S(1)}, bf16[2048,512]{1,0:T(8,128)(2,1)}, u32[]{:S(2)}) copy-start(bf16[2048,512]{1,0:T(8,128)(2,1)} %param.12) | copy-start | bytes 6291460
Sparse Core Ops, SparseCore 0:
  10.1 22.8 all-gather.6
  35.1 34.4 all-gather.8
  71.2 201.4 all-gather.12
  274.2 201.4 all-gather.14
  477.7 70.1 all-gather.10
  709.4 58.2 all-gather.16
  1283.3 77.7 reduce-scatter.3
  1363.6 51.1 reduce-scatter.5
  1671.6 71.3 reduce-scatter.7

commit v2 on v1

--- a/solution.py
+++ b/solution.py
@@ -45,15 +45,32 @@
     return part.reshape(*shape[:dim], shape[dim] // count, *shape[dim + 1 :])
 
 
-def to_offsets(blocked, seq_count):
+def swapped(spread, seq_count):
+    index = lax.axis_index("seq")
+    came = {}
+    for n in reversed(range(1, seq_count)):
+        piece = lax.dynamic_index_in_dim(spread, index ^ n, 0)
+        came[n] = lax.ppermute(piece, "seq", [(i, i ^ n) for i in range(seq_count)])
+    for n in range(1, seq_count):
+        spread = lax.dynamic_update_index_in_dim(spread, came[n], index ^ n, 0)
+    return spread
+
+
+def traded(spread, seq_count, by_permutes):
+    if by_permutes:
+        return swapped(spread, seq_count)
+    return lax.all_to_all(spread, "seq", split_axis=0, concat_axis=0, tiled=True)
+
+
+def to_offsets(blocked, seq_count, by_permutes=False):
     count, block_span, channels = blocked.shape
     places = block_span // seq_count
     split = blocked.reshape(count, seq_count, places, channels).transpose(1, 0, 2, 3)
-    return lax.all_to_all(split, "seq", split_axis=0, concat_axis=0, tiled=True)
-
-
-def to_blocks(spread, seq_count):
-    arrived = lax.all_to_all(spread, "seq", split_axis=0, concat_axis=0, tiled=True)
+    return traded(split, seq_count, by_permutes)
+
+
+def to_blocks(spread, seq_count, by_permutes=False):
+    arrived = traded(spread, seq_count, by_permutes)
     count, places, channels = arrived.shape[1:]
     return arrived.transpose(1, 0, 2, 3).reshape(count, seq_count * places, channels)
 
@@ -80,19 +97,19 @@
         return sides[:, :, None] == sides[:, None, :]
 
     weights, section_parts = [], []
-    for lo, hi in spans_of(IN_ONE, block_count):
+    for n, (lo, hi) in enumerate(spans_of(IN_ONE, block_count)):
         gathered = lax.all_gather(block_weight[lo:hi], "ch", axis=1, tiled=True)
         masked = jnp.where(mask_one(lo, hi), gathered, jnp.zeros_like(gathered))
         weights.append(gathered)
         section = jnp.einsum(
             "ikj,ijd->ikd", masked, inputs[lo:hi], preferred_element_type=jnp.float32
         ).astype(jnp.bfloat16)
-        section_parts.append(to_offsets(section, seq_count))
+        section_parts.append(to_offsets(section, seq_count, n > 0))
     full_weight = jnp.concatenate(weights, axis=0)
     section_spread = jnp.concatenate(section_parts, axis=1)
 
     full_grads, mixer_grads, grad_parts = [], [], []
-    for lo, hi in spans_of(IN_TWO, block_count):
+    for n, (lo, hi) in enumerate(spans_of(IN_TWO, block_count)):
         gathered = lax.all_gather(grads[lo:hi], "ch", axis=2, tiled=True)
         full_grads.append(gathered)
         head_grad = jnp.dot(
@@ -103,7 +120,7 @@
         sigmoid_gate = jax.nn.sigmoid(gates[lo:hi].astype(jnp.float32))
         mixer_grad = (head_grad * sigmoid_gate).astype(jnp.bfloat16)
         mixer_grads.append(mixer_grad)
-        grad_parts.append(to_offsets(mixer_grad, seq_count))
+        grad_parts.append(to_offsets(mixer_grad, seq_count, n > 0))
     grad_spread = jnp.concatenate(grad_parts, axis=1)
 
     own_offsets = lax.all_gather(offset_weight, "ch", axis=0, tiled=True)
@@ -118,7 +135,7 @@
     mixer_spread = mixer_spread.reshape(seq_count, block_count, places, channels)
     mixer_parts = []
     for lo, hi in spans_of(OUT_ONE, block_count):
-        mixer_parts.append(to_blocks(mixer_spread[:, lo:hi], seq_count))
+        mixer_parts.append(to_blocks(mixer_spread[:, lo:hi], seq_count, True))
     mixer_out = jnp.concatenate(mixer_parts)
     section_grad_spread = jnp.einsum(
         "kmi,mkd->ikd", masked_two, grad_spread, preferred_element_type=jnp.float32

time: 1850 us -> 2120 us (1.15)
  starting transfers between devices: 57.6 us -> 273 us
  local copies, waits for them, and re-layouts: 235 us -> 300 us
  waiting for transfers between devices: 1250 us -> 1220 us
    ppermute x0 -> x28, waiting for transfers between devices: none -> 600 us  [swapped(): came[n] = lax.ppermute(piece, 'seq', [(i, i ^ n) for i in range(seq_count)])]
    all_to_all x9 -> x5, waiting for transfers between devices: 827 us -> 259 us  [traded(): lax.all_to_all(spread, 'seq', split_axis=0, concat_axis=0, tiled=True)]
    ppermute x0 -> x28, starting transfers between devices: none -> 123 us  [swapped(): came[n] = lax.ppermute(piece, 'seq', [(i, i ^ n) for i in range(seq_count)])]
    all_to_all x9 -> x5, starting transfers between devices: 51.4 us -> 145 us  [traded(): lax.all_to_all(spread, 'seq', split_axis=0, concat_axis=0, tiled=True)]
    dynamic_update_slice x0 -> x28, local copies, waits for them, and re-layouts: none -> 63.1 us  [swapped(): spread = lax.dynamic_update_index_in_dim(spread, came[n], index ^ n, 0)]
    all_gather x3, waiting for transfers between devices: 43.1 us -> 0.01 us  [on_device(): gathered = lax.all_gather(block_weight[lo:hi], 'ch', axis=1, tiled=True)]
    all_gather x1, waiting for transfers between devices: 29.6 us -> 0.01 us  [on_device(): own_offsets = lax.all_gather(offset_weight, 'ch', axis=0, tiled=True)]
    all_gather x2, waiting for transfers between devices: 309 us -> 333 us  [on_device(): gathered = lax.all_gather(grads[lo:hi], 'ch', axis=2, tiled=True)]
  transfers between devices with their start and end apart: 23 -> 47, of which waited for: 14 -> 17; matrix products, arithmetic and copies ran while one was open for 28% -> 27% of each run, Pallas kernels for 0% -> 0%
where the time goes in v2:
time: 2120 us; the launch traced here: 2110 us
  waiting for transfers between devices  1220 us (58%)
  local copies, waits for them, and re-layouts  300 us (14%)
  starting transfers between devices  273 us (13%)
  matrix products  223 us (11%)
  other arithmetic  70.6 us (3%)
    ppermute x28, waiting for transfers between devices, swapped(): came[n] = lax.ppermute(piece, 'seq', [(i, i ^ n) for i in range(seq_count)])  600 us
    all_gather x2, waiting for transfers between devices, on_device(): gathered = lax.all_gather(grads[lo:hi], 'ch', axis=2, tiled=True)  333 us
    all_to_all x5, waiting for transfers between devices, traded(): lax.all_to_all(spread, 'seq', split_axis=0, concat_axis=0, tiled=True)  259 us
    all_to_all x5, starting transfers between devices, traded(): lax.all_to_all(spread, 'seq', split_axis=0, concat_axis=0, tiled=True)  145 us
    ppermute x28, starting transfers between devices, swapped(): came[n] = lax.ppermute(piece, 'seq', [(i, i ^ n) for i in range(seq_count)])  123 us
    dynamic_update_slice x28, local copies, waits for them, and re-layouts, swapped(): spread = lax.dynamic_update_index_in_dim(spread, came[n], index ^ n, 0)  63.1 us
    dot_general x2, matrix products, on_device(): jnp.dot(gathered.reshape(-1, out_weight.shape[0]), out_weight, preferred_...  58.2 us
    dot_general x1, matrix products, on_device(): jnp.einsum('te,tc->ec', full_grad, gated_out.reshape(token_count, channel...  46.2 us
  transfers between devices with their start and end apart: 47, of which 17 were waited for; matrix products, arithmetic and copies ran while one was open for 27% of the time, Pallas kernels for 0%

profile of v2, /device:TPU:6, one launch (start us, length us, event | category | flops | bytes accessed | tf_op | source)
XLA Modules:
  0.0 2105.9 jit_solution(1918830963651401756)
XLA Ops:
  7.2 11.7 fusion.70
  20.5 22.9 %add_divide_fusion.2 = (f32[8192,512]{1,0:T(8,128)}, f32[8192,512]{1,0:T(8,128)}) fusion(bf16[16384,512]{1,0:T(8,128)(2,1)} %param.8), kind=kLoop, calls=%fused_computation.22 | loop fusion | flops 33554432 | bytes 50331648 | tf_op jit(solution)/shard_map/div | solution.py:120
  43.3 177.6 %all-gather.13.cloned.1.call-done = bf16[16,512,2048]{2,1,0:T(8,128)(2,1)} async-done(((bf16[16,512,512]{2,1,0:T(8,128)(2,1)}), bf16[16,512,2048]{2,1,0:T(8,128)(2,1)}) %all-gather.13.cloned.1.call-update) | async-done | bytes 33554448 | tf_op jit(solution)/shard_map/all_gather | solution.py:113
  220.9 30.5 %multiply_convert_fusion.1 = bf16[16,512,512]{2,1,0:T(8,128)(2,1)} fusion(f32[16,512,512]{2,1,0:T(8,128)} %bitcast.173, bf16[16,512,2048]{2,1,0:T(8,128)(2,1)} %all-gather.13.cloned.1.call-done, bf16[2048,512]{1,0:T(8,128)(2,1)S(1)} %copy-done), kind=kOutput, calls=%fused_computation.21 | convolution fusion | flops 17188257792 | bytes 60817408 | tf_op jit(solution)/shard_map/dot_general | solution.py:115
  251.4 8.3 copy.105
  259.6 6.1 all-to-all-start
  268.4 155.6 %all-gather.15.cloned.1.call-done = bf16[16,512,2048]{2,1,0:T(8,128)(2,1)} async-done(((bf16[16,512,512]{2,1,0:T(8,128)(2,1)}), bf16[16,512,2048]{2,1,0:T(8,128)(2,1)}) %all-gather.15.cloned.1.call-update) | async-done | bytes 33554448 | tf_op jit(solution)/shard_map/all_gather | solution.py:113
  424.0 27.7 %multiply_convert_fusion = bf16[16,512,512]{2,1,0:T(8,128)(2,1)} fusion(f32[16,512,512]{2,1,0:T(8,128)} %bitcast.172, bf16[16,512,2048]{2,1,0:T(8,128)(2,1)} %all-gather.15.cloned.1.call-done, bf16[2048,512]{1,0:T(8,128)(2,1)S(1)} %copy-done), kind=kOutput, calls=%fused_computation.19 | convolution fusion | flops 17188257792 | bytes 60817408 | tf_op jit(solution)/shard_map/dot_general | solution.py:115
  451.8 5.7 dynamic-slice_bitcast_fusion.8
  466.7 16.3 collective-permute-done
  486.4 39.7 %collective-permute-done.1 = bf16[1,16,64,512]{3,2,1,0:T(8,128)(2,1)} collective-permute-done((bf16[1,16,64,512]{3,2,1,0:T(8,128)(2,1)}, bf16[1,16,64,512]{3,2,1,0:T(8,128)(2,1)}, u32[]{:S(2)}, u32[]{:S(2)}) %collective-permute-start.1) | collective-permute-done | bytes 1048608 | tf_op jit(solution)/shard_map/ppermute | solution.py:53
  529.5 9.2 copy.104
  543.2 5.7 collective-permute-done.2
  553.5 49.2 %collective-permute-done.4 = bf16[1,16,64,512]{3,2,1,0:T(8,128)(2,1)} collective-permute-done((bf16[1,16,64,512]{3,2,1,0:T(8,128)(2,1)}, bf16[1,16,64,512]{3,2,1,0:T(8,128)(2,1)}, u32[]{:S(2)}, u32[]{:S(2)}) %collective-permute-start.4) | collective-permute-done | bytes 1048608 | tf_op jit(solution)/shard_map/ppermute | solution.py:53
  609.6 8.0 pad_maximum_fusion
  617.6 21.2 %copy.57 = bf16[8,32,64,512]{3,1,0,2:T(8,128)(2,1)} copy(bf16[8,32,64,512]{3,2,1,0:T(8,128)(2,1)S(1)} %pad_maximum_fusion) | data formatting | bytes 33554432 | tf_op jit(solution)/shard_map/concatenate | solution.py:124
  638.8 18.1 convolution_convert_fusion.1
  657.0 10.7 slice.143
  667.7 13.5 copy.90
  681.2 43.7 %all-to-all-start.1 = ((bf16[8,18,64,512]{3,2,1,0:T(8,128)(2,1)}), bf16[8,18,64,512]{3,2,1,0:T(8,128)(2,1)}, u32[]{:S(2)}, u32[]{:S(2)}) async-start(bf16[8,18,64,512]{3,2,1,0:T(8,128)(2,1)} %copy.90), calls=%async_computation.1 | async-start | bytes 18874368 | tf_op jit(solution)/shard_map/all_to_all | solution.py:62
  727.0 9.6 slice.137
  736.5 192.6 %all-to-all-done.1 = bf16[8,18,64,512]{3,2,1,0:T(8,128)(2,1)} async-done(((bf16[8,18,64,512]{3,2,1,0:T(8,128)(2,1)}), bf16[8,18,64,512]{3,2,1,0:T(8,128)(2,1)}, u32[]{:S(2)}, u32[]{:S(2)}) %all-to-all-start.1) | async-done | bytes 9437216 | tf_op jit(solution)/shard_map/all_to_all | solution.py:62
  929.1 8.7 copy.62
  937.8 12.6 fusion.7
  950.4 13.5 slice.145
  963.9 9.3 copy.91
  973.2 6.1 all-to-all-start.2
  979.4 9.9 slice.135
  989.3 4.5 slice.132
  994.4 4.7 fusion.69
  999.0 5.8 fusion.36
  1014.4 13.8 fusion.19
  1028.2 7.0 dynamic-slice_bitcast_fusion
  1042.3 66.5 %all-to-all-done.2 = bf16[8,10,64,512]{3,2,1,0:T(8,128)(2,1)} async-done(((bf16[8,10,64,512]{3,2,1,0:T(8,128)(2,1)}), bf16[8,10,64,512]{3,2,1,0:T(8,128)(2,1)}, u32[]{:S(2)}, u32[]{:S(2)}) %all-to-all-start.2) | async-done | bytes 5242912 | tf_op jit(solution)/shard_map/all_to_all | solution.py:62
  1116.0 4.0 collective-permute-done.10
  1120.0 88.4 %collective-permute-done.11 = bf16[1,8,64,512]{3,2,0,1:T(8,128)(2,1)} collective-permute-done((bf16[1,8,64,512]{3,2,0,1:T(8,128)(2,1)}, bf16[1,8,64,512]{3,2,0,1:T(8,128)(2,1)}, u32[]{:S(2)}, u32[]{:S(2)}) %collective-permute-start.11) | collective-permute-done | bytes 524320 | tf_op jit(solution)/shard_map/ppermute | solution.py:53
  1208.4 12.2 collective-permute-start.17
  1222.5 21.1 %collective-permute-start.18 = (bf16[1,20,64,512]{3,2,0,1:T(8,128)(2,1)}, bf16[1,20,64,512]{3,2,0,1:T(8,128)(2,1)S(1)}, u32[]{:S(2)}, u32[]{:S(2)}) collective-permute-start(bf16[1,20,64,512]{3,2,0,1:T(8,128)(2,1)} %get-tuple-element.24), channel_id=1, source_target_pairs={{0,20},{4,16},{8,28},{12,24},{16,4},{20,0},{24,12},{28,8},{1,21},{... | collective-permute-start | bytes 3932168 | tf_op jit(solution)/shard_map/ppermute | solution.py:53
  1264.9 116.6 %collective-permute-done.17 = bf16[1,20,64,512]{3,2,0,1:T(8,128)(2,1)S(1)} collective-permute-done((bf16[1,20,64,512]{3,2,0,1:T(8,128)(2,1)}, bf16[1,20,64,512]{3,2,0,1:T(8,128)(2,1)S(1)}, u32[]{:S(2)}, u32[]{:S(2)}) %collective-permute-start.17) | collective-permute-done | bytes 1310752 | tf_op jit(solution)/shard_map/ppermute | solution.py:53
  1382.7 23.7 %collective-permute-done.18 = bf16[1,20,64,512]{3,2,0,1:T(8,128)(2,1)S(1)} collective-permute-done((bf16[1,20,64,512]{3,2,0,1:T(8,128)(2,1)}, bf16[1,20,64,512]{3,2,0,1:T(8,128)(2,1)S(1)}, u32[]{:S(2)}, u32[]{:S(2)}) %collective-permute-start.18) | collective-permute-done | bytes 1310752 | tf_op jit(solution)/shard_map/ppermute | solution.py:53
  1415.3 5.0 fusion.10
  1420.3 7.6 pad_maximum_fusion.1
  1427.9 21.3 %copy.72 = bf16[8,32,64,512]{3,1,0,2:T(8,128)(2,1)} copy(bf16[8,32,64,512]{3,2,0,1:T(8,128)(2,1)S(1)} %pad_maximum_fusion.1) | data formatting | bytes 33554432 | tf_op jit(solution)/shard_map/concatenate | solution.py:109
  1449.2 13.3 convolution_convert_fusion
  1462.5 15.6 copy.74
  1478.0 4.2 constant_dynamic-slice_fusion.9
  1482.2 6.5 copy-done.2
  1488.7 3.8 collective-permute-start.21
  1492.5 53.2 %collective-permute-start.22 = (bf16[1,32,64,512]{3,2,0,1:T(8,128)(2,1)S(1)}, bf16[1,32,64,512]{3,2,0,1:T(8,128)(2,1)S(1)}, u32[]{:S(2)}, u32[]{:S(2)}) collective-permute-start(bf16[1,32,64,512]{3,2,0,1:T(8,128)(2,1)S(1)} %get-tuple-element.16), channel_id=1, source_target_pairs={{0,8},{4,12},{8,0},{12,4},{16,24},{20,28},{24,16},{28,20},{1,9},{5... | collective-permute-start | bytes 6291464 | tf_op jit(solution)/shard_map/ppermute | solution.py:53
  1551.5 129.2 %collective-permute-done.22 = bf16[1,32,64,512]{3,2,0,1:T(8,128)(2,1)S(1)} collective-permute-done((bf16[1,32,64,512]{3,2,0,1:T(8,128)(2,1)S(1)}, bf16[1,32,64,512]{3,2,0,1:T(8,128)(2,1)S(1)}, u32[]{:S(2)}, u32[]{:S(2)}) %collective-permute-start.22) | collective-permute-done | bytes 2097184 | tf_op jit(solution)/shard_map/ppermute | solution.py:53
  1688.2 34.0 %collective-permute-done.23 = bf16[1,32,64,512]{3,2,0,1:T(8,128)(2,1)} collective-permute-done((bf16[1,32,64,512]{3,2,0,1:T(8,128)(2,1)}, bf16[1,32,64,512]{3,2,0,1:T(8,128)(2,1)}, u32[]{:S(2)}, u32[]{:S(2)}) %collective-permute-start.23) | collective-permute-done | bytes 2097184 | tf_op jit(solution)/shard_map/ppermute | solution.py:53
  1728.4 92.6 %collective-permute-done.25 = bf16[1,32,64,512]{3,2,0,1:T(8,128)(2,1)} collective-permute-done((bf16[1,32,64,512]{3,2,0,1:T(8,128)(2,1)}, bf16[1,32,64,512]{3,2,0,1:T(8,128)(2,1)}, u32[]{:S(2)}, u32[]{:S(2)}) %collective-permute-start.25) | collective-permute-done | bytes 2097184 | tf_op jit(solution)/shard_map/ppermute | solution.py:53
  1836.0 85.5 %all-to-all-start.3 = ((bf16[8,4,64,512]{3,1,2,0:T(4,128)(2,1)}), bf16[8,4,64,512]{3,1,2,0:T(4,128)(2,1)S(1)}, u32[]{:S(2)}, u32[]{:S(2)}) async-start(bf16[8,4,64,512]{3,1,2,0:T(4,128)(2,1)} %copy.92), calls=%async_computation.3 | async-start | bytes 4194304 | tf_op jit(solution)/shard_map/all_to_all | solution.py:62
  1921.5 15.9 fusion.8
  1937.4 46.2 %bitcast_convert_fusion = bf16[2048,512]{1,0:T(8,128)(2,1)S(1)} fusion(bf16[32,512,512]{2,1,0:T(8,128)(2,1)} %bitcast.152, bf16[32,512,512]{2,1,0:T(8,128)(2,1)} %bitcast.160, bf16[16,512,2048]{2,1,0:T(8,128)(2,1)} %all-gather.15.cloned.1.call-done, bf16[16,512,2048]{2,1,0:T(8,128)(2,1)} %all-gather.13.cloned.1.call-done), kind=kOutput, calls=%fused_computation.53 | convolution fusion | flops 34453061632 | bytes 102760448 | tf_op jit(solution)/shard_map/te,tc->ec/dot_general | solution.py:159
  1985.3 22.3 %collective-permute-done.30 = bf16[4,256,512]{2,1,0:T(8,128)(2,1)} collective-permute-done((bf16[4,256,512]{2,1,0:T(8,128)(2,1)S(1)}, bf16[4,256,512]{2,1,0:T(8,128)(2,1)}, u32[]{:S(2)}, u32[]{:S(2)}) %collective-permute-start.30) | collective-permute-done | bytes 1048608 | tf_op jit(solution)/shard_map/ppermute | solution.py:43
  2011.7 9.1 collective-permute-done.31
  2025.7 3.9 fusion.26
  2030.0 25.5 %fusion.5 = bf16[32,512,512]{2,1,0:T(8,128)(2,1)} fusion(bf16[32,512,512]{2,1,0:T(8,128)(2,1)} %bitcast.153, bf16[16,512,512]{2,1,0:T(8,128)(2,1)} %multiply_convert_fusion, bf16[16,512,512]{2,1,0:T(8,128)(2,1)} %multiply_convert_fusion.1, bf16[32,512,512]{2,1,0:T(8,128)(2,1)} %bitcast.161), kind=kLoop, calls=%fused_computation.7 | loop fusion | flops 92274688 | bytes 67108864 | tf_op jit(solution)/shard_map/convert_element_type | solution.py:156
  2057.6 14.2 fusion.18
  2071.8 6.1 dynamic_update_slice.113
  2077.9 8.1 convert_dynamic-update-slice_fusion
  2086.0 4.5 convert_dynamic-update-slice_fusion.1
  2090.5 4.2 dynamic_update_slice.137
  (192 shorter events, 148.0 us)
Async XLA Ops:
  7.2 213.8 %copy-start = (bf16[2048,512]{1,0:T(8,128)(2,1)S(1)}, bf16[2048,512]{1,0:T(8,128)(2,1)}, u32[]{:S(2)}) copy-start(bf16[2048,512]{1,0:T(8,128)(2,1)} %param.12) | copy-start | bytes 6291460
  7.2 213.7 %all-gather.13.cloned.1.call-start = ((), (), s32[]{:S(2)}) async-start(), calls=%async_computation.11 | async-start | bytes 41943040 | tf_op jit(solution)/shard_map/all_gather | solution.py:113
  19.0 405.0 %all-gather.15.cloned.1.call-start = ((), (), s32[]{:S(2)}) async-start(), calls=%async_computation.12 | async-start | bytes 41943040 | tf_op jit(solution)/shard_map/all_gather | solution.py:113
  19.7 619.1 %all-gather.17.cloned.1.call-start = ((), (), s32[]{:S(2)}) async-start(), calls=%async_computation.13 | async-start | bytes 10485760 | tf_op jit(solution)/shard_map/all_gather | solution.py:126
  259.6 350.0 %all-to-all-start = ((bf16[8,16,64,512]{3,2,1,0:T(8,128)(2,1)}), bf16[8,16,64,512]{3,2,1,0:T(8,128)(2,1)}, u32[]{:S(2)}, u32[]{:S(2)}) async-start(bf16[8,16,64,512]{3,2,1,0:T(8,128)(2,1)} %bitcast.164), calls=%async_computation | async-start | bytes 16777216 | tf_op jit(solution)/shard_map/all_to_all | solution.py:62
  265.7 733.3 %all-gather.9.cloned.1.call-start = ((), (), s32[]{:S(2)}) async-start(), calls=%async_computation.9 | async-start | bytes 5242880 | tf_op jit(solution)/shard_map/all_gather | solution.py:101
  268.1 746.3 %all-gather.11.cloned.1.call-start = ((), (), s32[]{:S(2)}) async-start(), calls=%async_computation.10 | async-start | bytes 13107200 | tf_op jit(solution)/shard_map/all_gather | solution.py:101
  451.8 7.8 copy-start.5
  451.8 9.6 copy-start.18
  457.5 25.5 %collective-permute-start = (bf16[1,16,64,512]{3,2,1,0:T(8,128)(2,1)}, bf16[1,16,64,512]{3,2,1,0:T(8,128)(2,1)}, u32[]{:S(2)}, u32[]{:S(2)}) collective-permute-start(bf16[1,16,64,512]{3,2,1,0:T(8,128)(2,1)} %get-tuple-element.35), channel_id=1, source_target_pairs={{0,4},{4,0},{8,12},{12,8},{16,20},{20,16},{24,28},{28,24},{1,5},{5... | collective-permute-start | bytes 3145736 | tf_op jit(solution)/shard_map/ppermute | solution.py:53
  458.2 67.9 %collective-permute-start.1 = (bf16[1,16,64,512]{3,2,1,0:T(8,128)(2,1)}, bf16[1,16,64,512]{3,2,1,0:T(8,128)(2,1)}, u32[]{:S(2)}, u32[]{:S(2)}) collective-permute-start(bf16[1,16,64,512]{3,2,1,0:T(8,128)(2,1)} %get-tuple-element.34), channel_id=1, source_target_pairs={{0,8},{4,12},{8,0},{12,4},{16,24},{20,28},{24,16},{28,20},{1,9},{5... | collective-permute-start | bytes 3145736 | tf_op jit(solution)/shard_map/ppermute | solution.py:53
  461.5 87.5 %collective-permute-start.2 = (bf16[1,16,64,512]{3,2,1,0:T(8,128)(2,1)}, bf16[1,16,64,512]{3,2,1,0:T(8,128)(2,1)}, u32[]{:S(2)}, u32[]{:S(2)}) collective-permute-start(bf16[1,16,64,512]{3,2,1,0:T(8,128)(2,1)} %get-tuple-element.33), channel_id=1, source_target_pairs={{0,12},{4,8},{8,4},{12,0},{16,28},{20,24},{24,20},{28,16},{1,13},{... | collective-permute-start | bytes 3145736 | tf_op jit(solution)/shard_map/ppermute | solution.py:53
  463.0 88.3 %collective-permute-start.3 = (bf16[1,16,64,512]{3,2,1,0:T(8,128)(2,1)}, bf16[1,16,64,512]{3,2,1,0:T(8,128)(2,1)}, u32[]{:S(2)}, u32[]{:S(2)}) collective-permute-start(bf16[1,16,64,512]{3,2,1,0:T(8,128)(2,1)} %get-tuple-element.32), channel_id=1, source_target_pairs={{0,16},{4,20},{8,24},{12,28},{16,0},{20,4},{24,8},{28,12},{1,17},{... | collective-permute-start | bytes 3145736 | tf_op jit(solution)/shard_map/ppermute | solution.py:53
  465.8 137.0 %collective-permute-start.4 = (bf16[1,16,64,512]{3,2,1,0:T(8,128)(2,1)}, bf16[1,16,64,512]{3,2,1,0:T(8,128)(2,1)}, u32[]{:S(2)}, u32[]{:S(2)}) collective-permute-start(bf16[1,16,64,512]{3,2,1,0:T(8,128)(2,1)} %get-tuple-element.31), channel_id=1, source_target_pairs={{0,20},{4,16},{8,28},{12,24},{16,4},{20,0},{24,12},{28,8},{1,21},{... | collective-permute-start | bytes 3145736 | tf_op jit(solution)/shard_map/ppermute | solution.py:53
  483.0 122.0 %collective-permute-start.5 = (bf16[1,16,64,512]{3,2,1,0:T(8,128)(2,1)S(1)}, bf16[1,16,64,512]{3,2,1,0:T(8,128)(2,1)}, u32[]{:S(2)}, u32[]{:S(2)}) collective-permute-start(bf16[1,16,64,512]{3,2,1,0:T(8,128)(2,1)S(1)} %get-tuple-element.30), channel_id=1, source_target_pairs={{0,24},{4,28},{8,16},{12,20},{16,8},{20,12},{24,0},{28,4},{1,25},{... | collective-permute-start | bytes 3145736 | tf_op jit(solution)/shard_map/ppermute | solution.py:53
  526.2 81.2 %collective-permute-start.6 = (bf16[1,16,64,512]{3,2,1,0:T(8,128)(2,1)S(1)}, bf16[1,16,64,512]{3,2,1,0:T(8,128)(2,1)}, u32[]{:S(2)}, u32[]{:S(2)}) collective-permute-start(bf16[1,16,64,512]{3,2,1,0:T(8,128)(2,1)S(1)} %get-tuple-element.29), channel_id=1, source_target_pairs={{0,28},{4,24},{8,20},{12,16},{16,12},{20,8},{24,4},{28,0},{1,29},{... | collective-permute-start | bytes 3145736 | tf_op jit(solution)/shard_map/ppermute | solution.py:53
  529.5 109.4 %copy-start.13 = (s32[64,256]{1,0:T(8,128)}, s32[64,256]{1,0:T(8,128)S(1)}, u32[]{:S(2)}) copy-start(s32[64,256]{1,0:T(8,128)S(1)} %copy.58) | copy-start | bytes 196612
  681.2 247.9 %all-to-all-start.1 = ((bf16[8,18,64,512]{3,2,1,0:T(8,128)(2,1)}), bf16[8,18,64,512]{3,2,1,0:T(8,128)(2,1)}, u32[]{:S(2)}, u32[]{:S(2)}) async-start(bf16[8,18,64,512]{3,2,1,0:T(8,128)(2,1)} %copy.90), calls=%async_computation.1 | async-start | bytes 18874368 | tf_op jit(solution)/shard_map/all_to_all | solution.py:62
  725.0 312.2 %all-gather.7.cloned.1.call-start = ((), (), s32[]{:S(2)}) async-start(), calls=%async_computation.8 | async-start | bytes 2621440 | tf_op jit(solution)/shard_map/all_gather | solution.py:101
  726.9 1363.6 %reduce-scatter.4.cloned.1.call-start = ((), (), s32[]{:S(2)}) async-start(), calls=%async_computation.14 | async-start | bytes 11796480 | tf_op jit(solution)/shard_map/reduce_scatter | solution.py:180
  736.5 201.2 %copy-start.16 = (pred[18,512]{1,0:T(8,128)(4,1)}, pred[18,512]{1,0:T(8,128)(4,1)S(1)}, u32[]{:S(2)}) copy-start(pred[18,512]{1,0:T(8,128)(4,1)S(1)} %constant_dynamic-slice_fusion.3) | copy-start | bytes 27652
  973.2 135.5 %all-to-all-start.2 = ((bf16[8,10,64,512]{3,2,1,0:T(8,128)(2,1)}), bf16[8,10,64,512]{3,2,1,0:T(8,128)(2,1)}, u32[]{:S(2)}, u32[]{:S(2)}) async-start(bf16[8,10,64,512]{3,2,1,0:T(8,128)(2,1)} %copy.91), calls=%async_computation.2 | async-start | bytes 10485760 | tf_op jit(solution)/shard_map/all_to_all | solution.py:62
  1008.5 27.3 %collective-permute-start.7 = (bf16[1,8,64,512]{3,2,0,1:T(8,128)(2,1)S(1)}, bf16[1,8,64,512]{3,2,0,1:T(8,128)(2,1)S(1)}, u32[]{:S(2)}, u32[]{:S(2)}) collective-permute-start(bf16[1,8,64,512]{3,2,0,1:T(8,128)(2,1)S(1)} %get-tuple-element.42), channel_id=1, source_target_pairs={{0,4},{4,0},{8,12},{12,8},{16,20},{20,16},{24,28},{28,24},{1,5},{5... | collective-permute-start | bytes 1572872 | tf_op jit(solution)/shard_map/ppermute | solution.py:53
  1008.6 103.8 %collective-permute-start.8 = (bf16[1,8,64,512]{3,2,0,1:T(8,128)(2,1)}, bf16[1,8,64,512]{3,2,0,1:T(8,128)(2,1)}, u32[]{:S(2)}, u32[]{:S(2)}) collective-permute-start(bf16[1,8,64,512]{3,2,0,1:T(8,128)(2,1)} %get-tuple-element.41), channel_id=1, source_target_pairs={{0,8},{4,12},{8,0},{12,4},{16,24},{20,28},{24,16},{28,20},{1,9},{5... | collective-permute-start | bytes 1572872 | tf_op jit(solution)/shard_map/ppermute | solution.py:53
  1010.6 104.0 %collective-permute-start.9 = (bf16[1,8,64,512]{3,2,0,1:T(8,128)(2,1)}, bf16[1,8,64,512]{3,2,0,1:T(8,128)(2,1)}, u32[]{:S(2)}, u32[]{:S(2)}) collective-permute-start(bf16[1,8,64,512]{3,2,0,1:T(8,128)(2,1)} %get-tuple-element.40), channel_id=1, source_target_pairs={{0,12},{4,8},{8,4},{12,0},{16,28},{20,24},{24,20},{28,16},{1,13},{... | collective-permute-start | bytes 1572872 | tf_op jit(solution)/shard_map/ppermute | solution.py:53
  1012.0 108.0 %collective-permute-start.10 = (bf16[1,8,64,512]{3,2,0,1:T(8,128)(2,1)}, bf16[1,8,64,512]{3,2,0,1:T(8,128)(2,1)}, u32[]{:S(2)}, u32[]{:S(2)}) collective-permute-start(bf16[1,8,64,512]{3,2,0,1:T(8,128)(2,1)} %get-tuple-element.39), channel_id=1, source_target_pairs={{0,16},{4,20},{8,24},{12,28},{16,0},{20,4},{24,8},{28,12},{1,17},{... | collective-permute-start | bytes 1572872 | tf_op jit(solution)/shard_map/ppermute | solution.py:53
  1035.2 210.3 %collective-permute-start.14 = (bf16[1,20,64,512]{3,2,0,1:T(8,128)(2,1)}, bf16[1,20,64,512]{3,2,0,1:T(8,128)(2,1)}, u32[]{:S(2)}, u32[]{:S(2)}) collective-permute-start(bf16[1,20,64,512]{3,2,0,1:T(8,128)(2,1)} %get-tuple-element.28), channel_id=1, source_target_pairs={{0,4},{4,0},{8,12},{12,8},{16,20},{20,16},{24,28},{28,24},{1,5},{5... | collective-permute-start | bytes 3932168 | tf_op jit(solution)/shard_map/ppermute | solution.py:53
  1035.8 214.0 %collective-permute-start.15 = (bf16[1,20,64,512]{3,2,0,1:T(8,128)(2,1)}, bf16[1,20,64,512]{3,2,0,1:T(8,128)(2,1)}, u32[]{:S(2)}, u32[]{:S(2)}) collective-permute-start(bf16[1,20,64,512]{3,2,0,1:T(8,128)(2,1)} %get-tuple-element.27), channel_id=1, source_target_pairs={{0,8},{4,12},{8,0},{12,4},{16,24},{20,28},{24,16},{28,20},{1,9},{5... | collective-permute-start | bytes 3932168 | tf_op jit(solution)/shard_map/ppermute | solution.py:53
  1108.8 311.5 %all-to-all-start.4 = ((bf16[8,4,64,512]{3,2,1,0:T(8,128)(2,1)}), bf16[8,4,64,512]{3,2,1,0:T(8,128)(2,1)S(1)}, u32[]{:S(2)}, u32[]{:S(2)}) async-start(bf16[8,4,64,512]{3,2,1,0:T(8,128)(2,1)} %bitcast.185), calls=%async_computation.4 | async-start | bytes 4194304 | tf_op jit(solution)/shard_map/all_to_all | solution.py:62
  1112.3 982.4 %reduce-scatter.6.cloned.1.call-start = ((), (), s32[]{:S(2)}) async-start(), calls=%async_computation.15 | async-start | bytes 6553600 | tf_op jit(solution)/shard_map/reduce_scatter | solution.py:180
  1112.4 96.0 %collective-permute-start.11 = (bf16[1,8,64,512]{3,2,0,1:T(8,128)(2,1)}, bf16[1,8,64,512]{3,2,0,1:T(8,128)(2,1)}, u32[]{:S(2)}, u32[]{:S(2)}) collective-permute-start(bf16[1,8,64,512]{3,2,0,1:T(8,128)(2,1)} %get-tuple-element.38), channel_id=1, source_target_pairs={{0,20},{4,16},{8,28},{12,24},{16,4},{20,0},{24,12},{28,8},{1,21},{... | collective-permute-start | bytes 1572872 | tf_op jit(solution)/shard_map/ppermute | solution.py:53
  1114.5 93.9 %collective-permute-start.12 = (bf16[1,8,64,512]{3,2,0,1:T(8,128)(2,1)}, bf16[1,8,64,512]{3,2,0,1:T(8,128)(2,1)}, u32[]{:S(2)}, u32[]{:S(2)}) collective-permute-start(bf16[1,8,64,512]{3,2,0,1:T(8,128)(2,1)} %get-tuple-element.37), channel_id=1, source_target_pairs={{0,24},{4,28},{8,16},{12,20},{16,8},{20,12},{24,0},{28,4},{1,25},{... | collective-permute-start | bytes 1572872 | tf_op jit(solution)/shard_map/ppermute | solution.py:53
  1120.0 102.5 %collective-permute-start.13 = (bf16[1,8,64,512]{3,2,0,1:T(8,128)(2,1)}, bf16[1,8,64,512]{3,2,0,1:T(8,128)(2,1)}, u32[]{:S(2)}, u32[]{:S(2)}) collective-permute-start(bf16[1,8,64,512]{3,2,0,1:T(8,128)(2,1)} %get-tuple-element.36), channel_id=1, source_target_pairs={{0,28},{4,24},{8,20},{12,16},{16,12},{20,8},{24,4},{28,0},{1,29},{... | collective-permute-start | bytes 1572872 | tf_op jit(solution)/shard_map/ppermute | solution.py:53
  1208.4 54.1 %collective-permute-start.16 = (bf16[1,20,64,512]{3,2,0,1:T(8,128)(2,1)}, bf16[1,20,64,512]{3,2,0,1:T(8,128)(2,1)}, u32[]{:S(2)}, u32[]{:S(2)}) collective-permute-start(bf16[1,20,64,512]{3,2,0,1:T(8,128)(2,1)} %get-tuple-element.26), channel_id=1, source_target_pairs={{0,12},{4,8},{8,4},{12,0},{16,28},{20,24},{24,20},{28,16},{1,13},{... | collective-permute-start | bytes 3932168 | tf_op jit(solution)/shard_map/ppermute | solution.py:53
  1208.4 204.6 %copy-start.19 = (pred[10,512]{1,0:T(8,128)(4,1)}, pred[10,512]{1,0:T(8,128)(4,1)S(1)}, u32[]{:S(2)}) copy-start(pred[10,512]{1,0:T(8,128)(4,1)S(1)} %constant_dynamic-slice_fusion.2) | copy-start | bytes 15364
  1208.4 173.1 %collective-permute-start.17 = (bf16[1,20,64,512]{3,2,0,1:T(8,128)(2,1)}, bf16[1,20,64,512]{3,2,0,1:T(8,128)(2,1)S(1)}, u32[]{:S(2)}, u32[]{:S(2)}) collective-permute-start(bf16[1,20,64,512]{3,2,0,1:T(8,128)(2,1)} %get-tuple-element.25), channel_id=1, source_target_pairs={{0,16},{4,20},{8,24},{12,28},{16,0},{20,4},{24,8},{28,12},{1,17},{... | collective-permute-start | bytes 3932168 | tf_op jit(solution)/shard_map/ppermute | solution.py:53
  1222.5 184.0 %collective-permute-start.18 = (bf16[1,20,64,512]{3,2,0,1:T(8,128)(2,1)}, bf16[1,20,64,512]{3,2,0,1:T(8,128)(2,1)S(1)}, u32[]{:S(2)}, u32[]{:S(2)}) collective-permute-start(bf16[1,20,64,512]{3,2,0,1:T(8,128)(2,1)} %get-tuple-element.24), channel_id=1, source_target_pairs={{0,20},{4,16},{8,28},{12,24},{16,4},{20,0},{24,12},{28,8},{1,21},{... | collective-permute-start | bytes 3932168 | tf_op jit(solution)/shard_map/ppermute | solution.py:53
  1245.4 162.2 %collective-permute-start.19 = (bf16[1,20,64,512]{3,2,0,1:T(8,128)(2,1)}, bf16[1,20,64,512]{3,2,0,1:T(8,128)(2,1)S(1)}, u32[]{:S(2)}, u32[]{:S(2)}) collective-permute-start(bf16[1,20,64,512]{3,2,0,1:T(8,128)(2,1)} %get-tuple-element.23), channel_id=1, source_target_pairs={{0,24},{4,28},{8,16},{12,20},{16,8},{20,12},{24,0},{28,4},{1,25},{... | collective-permute-start | bytes 3932168 | tf_op jit(solution)/shard_map/ppermute | solution.py:53
  1249.7 159.0 %collective-permute-start.20 = (bf16[1,20,64,512]{3,2,0,1:T(8,128)(2,1)S(1)}, bf16[1,20,64,512]{3,2,0,1:T(8,128)(2,1)S(1)}, u32[]{:S(2)}, u32[]{:S(2)}) collective-permute-start(bf16[1,20,64,512]{3,2,0,1:T(8,128)(2,1)S(1)} %get-tuple-element.22), channel_id=1, source_target_pairs={{0,28},{4,24},{8,20},{12,16},{16,12},{20,8},{24,4},{28,0},{1,29},{... | collective-permute-start | bytes 3932168 | tf_op jit(solution)/shard_map/ppermute | solution.py:53
  1407.6 7.7 slice-start
  1420.3 28.9 %slice-start.1 = ((s8[8388608]{0:T(1024)(128)(4,1)}), s8[4194304]{0:T(1024)(128)(4,1)S(1)}, s32[]{:S(2)}) async-start(s8[8388608]{0:T(1024)(128)(4,1)} %bitcast.177), calls=%async_computation.18 | async-start | bytes 8388608
  1427.9 21.3 %slice-start.2 = ((s8[8388608]{0:T(1024)(128)(4,1)}), s8[4194304]{0:T(1024)(128)(4,1)S(1)}, s32[]{:S(2)}) async-start(s8[8388608]{0:T(1024)(128)(4,1)} %bitcast.177), calls=%async_computation.19 | async-start | bytes 8388608
  1427.9 21.3 %copy-start.14 = (s32[64,256]{1,0:T(8,128)S(1)}, s32[64,256]{1,0:T(8,128)}, u32[]{:S(2)}) copy-start(s32[64,256]{1,0:T(8,128)} %copy-done.13) | copy-start | bytes 196612
  1478.0 10.7 copy-start.2
  1488.7 60.8 %collective-permute-start.21 = (bf16[1,32,64,512]{3,2,0,1:T(8,128)(2,1)S(1)}, bf16[1,32,64,512]{3,2,0,1:T(8,128)(2,1)S(1)}, u32[]{:S(2)}, u32[]{:S(2)}) collective-permute-start(bf16[1,32,64,512]{3,2,0,1:T(8,128)(2,1)S(1)} %get-tuple-element.17), channel_id=1, source_target_pairs={{0,4},{4,0},{8,12},{12,8},{16,20},{20,16},{24,28},{28,24},{1,5},{5... | collective-permute-start | bytes 6291464 | tf_op jit(solution)/shard_map/ppermute | solution.py:53
  1492.5 188.2 %collective-permute-start.22 = (bf16[1,32,64,512]{3,2,0,1:T(8,128)(2,1)S(1)}, bf16[1,32,64,512]{3,2,0,1:T(8,128)(2,1)S(1)}, u32[]{:S(2)}, u32[]{:S(2)}) collective-permute-start(bf16[1,32,64,512]{3,2,0,1:T(8,128)(2,1)S(1)} %get-tuple-element.16), channel_id=1, source_target_pairs={{0,8},{4,12},{8,0},{12,4},{16,24},{20,28},{24,16},{28,20},{1,9},{5... | collective-permute-start | bytes 6291464 | tf_op jit(solution)/shard_map/ppermute | solution.py:53
  1545.7 176.5 %collective-permute-start.23 = (bf16[1,32,64,512]{3,2,0,1:T(8,128)(2,1)}, bf16[1,32,64,512]{3,2,0,1:T(8,128)(2,1)}, u32[]{:S(2)}, u32[]{:S(2)}) collective-permute-start(bf16[1,32,64,512]{3,2,0,1:T(8,128)(2,1)} %get-tuple-element.15), channel_id=1, source_target_pairs={{0,12},{4,8},{8,4},{12,0},{16,28},{20,24},{24,20},{28,16},{1,13},{... | collective-permute-start | bytes 6291464 | tf_op jit(solution)/shard_map/ppermute | solution.py:53
  1545.7 179.6 %collective-permute-start.24 = (bf16[1,32,64,512]{3,2,0,1:T(8,128)(2,1)}, bf16[1,32,64,512]{3,2,0,1:T(8,128)(2,1)}, u32[]{:S(2)}, u32[]{:S(2)}) collective-permute-start(bf16[1,32,64,512]{3,2,0,1:T(8,128)(2,1)} %get-tuple-element.14), channel_id=1, source_target_pairs={{0,16},{4,20},{8,24},{12,28},{16,0},{20,4},{24,8},{28,12},{1,17},{... | collective-permute-start | bytes 6291464 | tf_op jit(solution)/shard_map/ppermute | solution.py:53
  1547.7 273.4 %collective-permute-start.25 = (bf16[1,32,64,512]{3,2,0,1:T(8,128)(2,1)}, bf16[1,32,64,512]{3,2,0,1:T(8,128)(2,1)}, u32[]{:S(2)}, u32[]{:S(2)}) collective-permute-start(bf16[1,32,64,512]{3,2,0,1:T(8,128)(2,1)} %get-tuple-element.13), channel_id=1, source_target_pairs={{0,20},{4,16},{8,28},{12,24},{16,4},{20,0},{24,12},{28,8},{1,21},{... | collective-permute-start | bytes 6291464 | tf_op jit(solution)/shard_map/ppermute | solution.py:53
  1549.6 131.1 %copy-start.9 = (bf16[1,32,64,512]{3,2,0,1:T(8,128)(2,1)}, bf16[1,32,64,512]{3,2,0,1:T(8,128)(2,1)S(1)}, u32[]{:S(2)}) copy-start(bf16[1,32,64,512]{3,2,0,1:T(8,128)(2,1)S(1)} %collective-permute-done.21) | copy-start | bytes 6291460
  1549.6 274.6 %collective-permute-start.26 = (bf16[1,32,64,512]{3,2,0,1:T(8,128)(2,1)}, bf16[1,32,64,512]{3,2,0,1:T(8,128)(2,1)}, u32[]{:S(2)}, u32[]{:S(2)}) collective-permute-start(bf16[1,32,64,512]{3,2,0,1:T(8,128)(2,1)} %get-tuple-element.12), channel_id=1, source_target_pairs={{0,24},{4,28},{8,16},{12,20},{16,8},{20,12},{24,0},{28,4},{1,25},{... | collective-permute-start | bytes 6291464 | tf_op jit(solution)/shard_map/ppermute | solution.py:53
  1682.0 145.3 %collective-permute-start.27 = (bf16[1,32,64,512]{3,2,0,1:T(8,128)(2,1)S(1)}, bf16[1,32,64,512]{3,2,0,1:T(8,128)(2,1)}, u32[]{:S(2)}, u32[]{:S(2)}) collective-permute-start(bf16[1,32,64,512]{3,2,0,1:T(8,128)(2,1)S(1)} %get-tuple-element.11), channel_id=1, source_target_pairs={{0,28},{4,24},{8,20},{12,16},{16,12},{20,8},{24,4},{28,0},{1,29},{... | collective-permute-start | bytes 6291464 | tf_op jit(solution)/shard_map/ppermute | solution.py:53
  1836.0 189.2 %all-to-all-start.3 = ((bf16[8,4,64,512]{3,1,2,0:T(4,128)(2,1)}), bf16[8,4,64,512]{3,1,2,0:T(4,128)(2,1)S(1)}, u32[]{:S(2)}, u32[]{:S(2)}) async-start(bf16[8,4,64,512]{3,1,2,0:T(4,128)(2,1)} %copy.92), calls=%async_computation.3 | async-start | bytes 4194304 | tf_op jit(solution)/shard_map/all_to_all | solution.py:62
  1921.5 177.7 %reduce-scatter.8.cloned.1.call-start = ((), (), s32[]{:S(2)}) async-start(), calls=%async_computation.16 | async-start | bytes 10485760 | tf_op jit(solution)/shard_map/reduce_scatter | solution.py:148
  1983.6 42.1 %copy-start.21 = (pred[4,512]{1,0:T(4,128)(4,1)S(1)}, pred[4,512]{1,0:T(4,128)(4,1)}, u32[]{:S(2)}) copy-start(pred[4,512]{1,0:T(4,128)(4,1)} %get-tuple-element.46) | copy-start | bytes 6148
  1985.0 22.6 %collective-permute-start.30 = (bf16[4,256,512]{2,1,0:T(8,128)(2,1)S(1)}, bf16[4,256,512]{2,1,0:T(8,128)(2,1)}, u32[]{:S(2)}, u32[]{:S(2)}) collective-permute-start(bf16[4,256,512]{2,1,0:T(8,128)(2,1)S(1)} %dynamic-slice_bitcast_fusion.7), channel_id=1, source_target_pairs={{0,4},{4,0},{8,12},{12,8},{16,20},{20,16},{24,28},{28,24},{1,5},{5... | collective-permute-start | bytes 3145736 | tf_op jit(solution)/shard_map/ppermute | solution.py:43
  2010.2 10.6 collective-permute-start.31
  2022.8 32.7 %collective-permute-start.32 = (bf16[1,256,512]{2,1,0:T(8,128)(2,1)S(1)}, bf16[1,256,512]{2,1,0:T(8,128)(2,1)S(1)}, u32[]{:S(2)}, u32[]{:S(2)}) collective-permute-start(bf16[1,256,512]{2,1,0:T(8,128)(2,1)S(1)} %constant_dynamic-slice_fusion.4), channel_id=1, source_target_pairs={{0,16},{4,20},{8,24},{12,28},{16,0},{20,4},{24,8},{28,12},{1,17},{... | collective-permute-start | bytes 786440 | tf_op jit(solution)/shard_map/ppermute | solution.py:43
  2029.9 25.6 %copy-start.12 = (bf16[2,256,512]{2,1,0:T(8,128)(2,1)S(1)}, bf16[2,256,512]{2,1,0:T(8,128)(2,1)}, u32[]{:S(2)}) copy-start(bf16[2,256,512]{2,1,0:T(8,128)(2,1)} %copy-done.11) | copy-start | bytes 1572868
  2029.9 27.7 %copy-start.17 = (pred[18,512]{1,0:T(8,128)(4,1)S(1)}, pred[18,512]{1,0:T(8,128)(4,1)}, u32[]{:S(2)}) copy-start(pred[18,512]{1,0:T(8,128)(4,1)} %copy-done.16) | copy-start | bytes 27652
  2029.9 26.3 %collective-permute-start.28 = (bf16[4,2,128,512]{3,2,0,1:T(8,128)(2,1)S(1)}, bf16[4,2,128,512]{3,2,0,1:T(8,128)(2,1)S(1)}, u32[]{:S(2)}, u32[]{:S(2)}) collective-permute-start(bf16[4,2,128,512]{3,2,0,1:T(8,128)(2,1)S(1)} %bitcast.200), channel_id=1, source_target_pairs={{0,1},{1,0},{2,3},{3,2},{4,5},{5,4},{6,7},{7,6},{8,9},{9,8},{10,11... | collective-permute-start | bytes 3145736 | tf_op jit(solution)/shard_map/ppermute | solution.py:43
  2057.4 39.8 %collective-permute-start.29 = (bf16[4,1,128,512]{3,2,0,1:T(8,128)(2,1)}, bf16[4,1,128,512]{3,2,0,1:T(8,128)(2,1)}, u32[]{:S(2)}, u32[]{:S(2)}) collective-permute-start(bf16[4,1,128,512]{3,2,0,1:T(8,128)(2,1)} %constant_dynamic-slice_fusion.5), channel_id=1, source_target_pairs={{0,2},{1,3},{2,0},{3,1},{4,6},{5,7},{6,4},{7,5},{8,10},{9,11},{10,... | collective-permute-start | bytes 1572872 | tf_op jit(solution)/shard_map/ppermute | solution.py:43
  2077.9 8.1 copy-start.8
  2077.9 21.2 %copy-start.1 = (bf16[2048,512]{1,0:T(8,128)(2,1)S(1)}, bf16[2048,512]{1,0:T(8,128)(2,1)}, u32[]{:S(2)}) copy-start(bf16[2048,512]{1,0:T(8,128)(2,1)} %param.12) | copy-start | bytes 6291460
  (8 other events, 19.6 us)
Sparse Core Ops, SparseCore 0:
  19.1 201.7 all-gather.12
  222.5 201.4 all-gather.14
  425.6 58.2 all-gather.16
  485.3 34.4 all-gather.8
  521.2 70.1 all-gather.10
  727.0 22.4 all-gather.6
  950.5 75.5 reduce-scatter.3
  1420.4 104.9 reduce-scatter.5
  1937.5 71.2 reduce-scatter.7

commit v3 on v2

--- a/solution.py
+++ b/solution.py
@@ -4,10 +4,10 @@
 from jax.sharding import PartitionSpec as P
 
 
-IN_ONE = (2, 4, 10)
+IN_ONE = (1, 2, 4, 9)
 IN_TWO = (8, 8)
 OUT_ONE = (16,)
-OUT_TWO = (9, 5, 2)
+OUT_TWO = (9, 4, 2, 1)
 
 
 def side_flags_of(reset_offset, block_span):
@@ -26,7 +26,7 @@
     for share in shares:
         cuts.append(cuts[-1] + share)
     cuts = [cut * block_count // 16 for cut in cuts]
-    return list(zip(cuts, cuts[1:]))
+    return [span for span in zip(cuts, cuts[1:]) if span[0] < span[1]]
 
 
 def scatter_sum(part, axis_name, dim):
@@ -174,7 +174,7 @@
         )
         partial_grad = jnp.where(mask, partial_grad, jnp.zeros_like(partial_grad))
         partial_grad = partial_grad.astype(jnp.bfloat16)
-        if n == len(OUT_TWO) - 1:
+        if n > 1:
             reduced = scatter_sum(partial_grad, "ch", 1)
         else:
             reduced = lax.psum_scatter(partial_grad, "ch", scatter_dimension=1, tiled=True)

time: 2120 us -> 2120 us (level)
  starting transfers between devices: 273 us -> 334 us
  waiting for transfers between devices: 1220 us -> 1180 us
    all_to_all x5 -> x6, waiting for transfers between devices: 259 us -> 194 us  [traded(): lax.all_to_all(spread, 'seq', split_axis=0, concat_axis=0, tiled=True)]
    ppermute x28 -> x35, starting transfers between devices: 123 us -> 174 us  [swapped(): came[n] = lax.ppermute(piece, 'seq', [(i, i ^ n) for i in range(seq_count)])]
    dynamic_update_slice x28 -> x35, local copies, waits for them, and re-layouts: 63.1 us -> 49.2 us  [swapped(): spread = lax.dynamic_update_index_in_dim(spread, came[n], index ^ n, 0)]
    ppermute x28 -> x35, waiting for transfers between devices: 600 us -> 612 us  [swapped(): came[n] = lax.ppermute(piece, 'seq', [(i, i ^ n) for i in range(seq_count)])]
    all_to_all x5 -> x6, starting transfers between devices: 145 us -> 153 us  [traded(): lax.all_to_all(spread, 'seq', split_axis=0, concat_axis=0, tiled=True)]
  transfers between devices with their start and end apart: 47 -> 58, of which waited for: 17 -> 20; matrix products, arithmetic and copies ran while one was open for 27% -> 27% of each run, Pallas kernels for 0% -> 0%
where the time goes in v3:
time: 2120 us; the launch traced here: 2110 us
  waiting for transfers between devices  1180 us (56%)
  starting transfers between devices  334 us (16%)
  local copies, waits for them, and re-layouts  289 us (14%)
  matrix products  233 us (11%)
  other arithmetic  67.9 us (3%)
    ppermute x35, waiting for transfers between devices, swapped(): came[n] = lax.ppermute(piece, 'seq', [(i, i ^ n) for i in range(seq_count)])  612 us
    all_gather x2, waiting for transfers between devices, on_device(): gathered = lax.all_gather(grads[lo:hi], 'ch', axis=2, tiled=True)  332 us
    all_to_all x6, waiting for transfers between devices, traded(): lax.all_to_all(spread, 'seq', split_axis=0, concat_axis=0, tiled=True)  194 us
    ppermute x35, starting transfers between devices, swapped(): came[n] = lax.ppermute(piece, 'seq', [(i, i ^ n) for i in range(seq_count)])  174 us
    all_to_all x6, starting transfers between devices, traded(): lax.all_to_all(spread, 'seq', split_axis=0, concat_axis=0, tiled=True)  153 us
    dot_general x2, matrix products, on_device(): jnp.dot(gathered.reshape(-1, out_weight.shape[0]), out_weight, preferred_...  58.3 us
    dynamic_update_slice x35, local copies, waits for them, and re-layouts, swapped(): spread = lax.dynamic_update_index_in_dim(spread, came[n], index ^ n, 0)  49.2 us
    dot_general x1, matrix products, on_device(): jnp.einsum('te,tc->ec', full_grad, gated_out.reshape(token_count, channel...  44.2 us
  transfers between devices with their start and end apart: 58, of which 20 were waited for; matrix products, arithmetic and copies ran while one was open for 27% of the time, Pallas kernels for 0%

profile of v3, /device:TPU:6, one launch (start us, length us, event | category | flops | bytes accessed | tf_op | source)
XLA Modules:
  0.0 2114.1 jit_solution(2418358081900379494)
XLA Ops:
  7.2 11.7 fusion.87
  20.4 22.9 %add_divide_fusion.2 = (f32[8192,512]{1,0:T(8,128)}, f32[8192,512]{1,0:T(8,128)}) fusion(bf16[16384,512]{1,0:T(8,128)(2,1)} %param.8), kind=kLoop, calls=%fused_computation.22 | loop fusion | flops 33554432 | bytes 50331648 | tf_op jit(solution)/shard_map/div | solution.py:120
  43.3 177.6 %all-gather.16.cloned.1.call-done = bf16[16,512,2048]{2,1,0:T(8,128)(2,1)} async-done(((bf16[16,512,512]{2,1,0:T(8,128)(2,1)}), bf16[16,512,2048]{2,1,0:T(8,128)(2,1)}) %all-gather.16.cloned.1.call-update) | async-done | bytes 33554448 | tf_op jit(solution)/shard_map/all_gather | solution.py:113
  220.9 30.5 %multiply_convert_fusion.1 = bf16[16,512,512]{2,1,0:T(8,128)(2,1)} fusion(f32[16,512,512]{2,1,0:T(8,128)} %bitcast.213, bf16[16,512,2048]{2,1,0:T(8,128)(2,1)} %all-gather.16.cloned.1.call-done, bf16[2048,512]{1,0:T(8,128)(2,1)S(1)} %copy-done), kind=kOutput, calls=%fused_computation.21 | convolution fusion | flops 17188257792 | bytes 60817408 | tf_op jit(solution)/shard_map/dot_general | solution.py:115
  251.3 8.4 copy.123
  259.7 6.1 all-to-all-start
  269.7 154.3 %all-gather.18.cloned.1.call-done = bf16[16,512,2048]{2,1,0:T(8,128)(2,1)} async-done(((bf16[16,512,512]{2,1,0:T(8,128)(2,1)}), bf16[16,512,2048]{2,1,0:T(8,128)(2,1)}) %all-gather.18.cloned.1.call-update) | async-done | bytes 33554448 | tf_op jit(solution)/shard_map/all_gather | solution.py:113
  424.0 27.8 %multiply_convert_fusion = bf16[16,512,512]{2,1,0:T(8,128)(2,1)} fusion(f32[16,512,512]{2,1,0:T(8,128)} %bitcast.212, bf16[16,512,2048]{2,1,0:T(8,128)(2,1)} %all-gather.18.cloned.1.call-done, bf16[2048,512]{1,0:T(8,128)(2,1)S(1)} %copy-done), kind=kOutput, calls=%fused_computation.19 | convolution fusion | flops 17188257792 | bytes 60817408 | tf_op jit(solution)/shard_map/dot_general | solution.py:115
  451.8 5.6 dynamic-slice_bitcast_fusion.8
  467.1 15.8 collective-permute-done
  486.3 39.3 %collective-permute-done.1 = bf16[1,16,64,512]{3,2,1,0:T(8,128)(2,1)} collective-permute-done((bf16[1,16,64,512]{3,2,1,0:T(8,128)(2,1)}, bf16[1,16,64,512]{3,2,1,0:T(8,128)(2,1)}, u32[]{:S(2)}, u32[]{:S(2)}) %collective-permute-start.1) | collective-permute-done | bytes 1048608 | tf_op jit(solution)/shard_map/ppermute | solution.py:53
  528.8 8.0 copy.122
  541.5 6.8 collective-permute-done.2
  552.8 50.3 %collective-permute-done.4 = bf16[1,16,64,512]{3,2,1,0:T(8,128)(2,1)} collective-permute-done((bf16[1,16,64,512]{3,2,1,0:T(8,128)(2,1)}, bf16[1,16,64,512]{3,2,1,0:T(8,128)(2,1)}, u32[]{:S(2)}, u32[]{:S(2)}) %collective-permute-start.4) | collective-permute-done | bytes 1048608 | tf_op jit(solution)/shard_map/ppermute | solution.py:53
  610.1 8.0 pad_maximum_fusion
  618.0 21.2 %copy.63 = bf16[8,32,64,512]{3,1,0,2:T(8,128)(2,1)} copy(bf16[8,32,64,512]{3,2,1,0:T(8,128)(2,1)S(1)} %pad_maximum_fusion) | data formatting | bytes 33554432 | tf_op jit(solution)/shard_map/concatenate | solution.py:124
  639.3 18.1 convolution_convert_fusion.1
  657.4 10.7 slice.179
  668.1 13.5 copy.102
  681.7 43.7 %all-to-all-start.1 = ((bf16[8,18,64,512]{3,2,1,0:T(8,128)(2,1)}), bf16[8,18,64,512]{3,2,1,0:T(8,128)(2,1)}, u32[]{:S(2)}, u32[]{:S(2)}) async-start(bf16[8,18,64,512]{3,2,1,0:T(8,128)(2,1)} %copy.102), calls=%async_computation.1 | async-start | bytes 18874368 | tf_op jit(solution)/shard_map/all_to_all | solution.py:62
  729.0 15.5 fusion.86
  744.5 185.0 %all-to-all-done.1 = bf16[8,18,64,512]{3,2,1,0:T(8,128)(2,1)} async-done(((bf16[8,18,64,512]{3,2,1,0:T(8,128)(2,1)}), bf16[8,18,64,512]{3,2,1,0:T(8,128)(2,1)}, u32[]{:S(2)}, u32[]{:S(2)}) %all-to-all-start.1) | async-done | bytes 9437216 | tf_op jit(solution)/shard_map/all_to_all | solution.py:62
  929.5 8.6 copy.68
  938.1 12.6 fusion.7
  954.7 8.5 fusion.85
  966.6 5.3 all-to-all-start.5
  971.9 5.0 fusion.84
  987.5 7.1 fusion.36
  994.6 5.0 slice.181
  1002.0 6.4 all-to-all-start.2
  1016.1 13.1 fusion.19
  1032.2 57.4 %collective-permute-done.12 = bf16[1,4,64,512]{3,2,0,1:T(8,128)(2,1)} collective-permute-done((bf16[1,4,64,512]{3,2,0,1:T(8,128)(2,1)}, bf16[1,4,64,512]{3,2,0,1:T(8,128)(2,1)}, u32[]{:S(2)}, u32[]{:S(2)}) %collective-permute-start.12) | collective-permute-done | bytes 262176 | tf_op jit(solution)/shard_map/ppermute | solution.py:53
  1089.6 38.1 %collective-permute-start.17 = (bf16[1,8,64,512]{3,2,0,1:T(8,128)(2,1)S(1)}, bf16[1,8,64,512]{3,2,0,1:T(8,128)(2,1)S(1)}, u32[]{:S(2)}, u32[]{:S(2)}) collective-permute-start(bf16[1,8,64,512]{3,2,0,1:T(8,128)(2,1)S(1)} %copy-done.21), channel_id=1, source_target_pairs={{0,16},{4,20},{8,24},{12,28},{16,0},{20,4},{24,8},{28,12},{1,17},{... | collective-permute-start | bytes 1572872 | tf_op jit(solution)/shard_map/ppermute | solution.py:53
  1127.8 7.2 dynamic-slice_bitcast_fusion
  1136.8 9.6 collective-permute-start.18
  1153.6 12.9 collective-permute-done.17
  1168.0 10.7 collective-permute-done.18
  1178.7 21.1 collective-permute-done.19
  1199.8 12.1 collective-permute-start.24
  1214.1 21.1 collective-permute-start.25
  1238.8 15.4 collective-permute-done.23
  1254.4 103.3 %collective-permute-done.24 = bf16[1,18,64,512]{3,2,0,1:T(8,128)(2,1)S(1)} collective-permute-done((bf16[1,18,64,512]{3,2,0,1:T(8,128)(2,1)}, bf16[1,18,64,512]{3,2,0,1:T(8,128)(2,1)S(1)}, u32[]{:S(2)}, u32[]{:S(2)}) %collective-permute-start.24) | collective-permute-done | bytes 1179680 | tf_op jit(solution)/shard_map/ppermute | solution.py:53
  1357.8 24.3 %collective-permute-done.25 = bf16[1,18,64,512]{3,2,0,1:T(8,128)(2,1)S(1)} collective-permute-done((bf16[1,18,64,512]{3,2,0,1:T(8,128)(2,1)}, bf16[1,18,64,512]{3,2,0,1:T(8,128)(2,1)S(1)}, u32[]{:S(2)}, u32[]{:S(2)}) %collective-permute-start.25) | collective-permute-done | bytes 1179680 | tf_op jit(solution)/shard_map/ppermute | solution.py:53
  1384.5 21.3 %copy.81 = bf16[8,32,64,512]{3,1,0,2:T(8,128)(2,1)} copy(bf16[8,32,64,512]{3,2,0,1:T(8,128)(2,1)S(1)} %pad_maximum_fusion.1) | data formatting | bytes 33554432 | tf_op jit(solution)/shard_map/concatenate | solution.py:109
  1415.6 17.2 convolution_convert_fusion
  1432.8 15.6 copy.83
  1452.5 4.2 copy-done.2
  1459.0 50.6 %collective-permute-start.29 = (bf16[1,32,64,512]{3,2,0,1:T(8,128)(2,1)S(1)}, bf16[1,32,64,512]{3,2,0,1:T(8,128)(2,1)S(1)}, u32[]{:S(2)}, u32[]{:S(2)}) collective-permute-start(bf16[1,32,64,512]{3,2,0,1:T(8,128)(2,1)S(1)} %get-tuple-element.22), channel_id=1, source_target_pairs={{0,8},{4,12},{8,0},{12,4},{16,24},{20,28},{24,16},{28,20},{1,9},{5... | collective-permute-start | bytes 6291464 | tf_op jit(solution)/shard_map/ppermute | solution.py:53
  1517.5 127.9 %collective-permute-done.29 = bf16[1,32,64,512]{3,2,0,1:T(8,128)(2,1)S(1)} collective-permute-done((bf16[1,32,64,512]{3,2,0,1:T(8,128)(2,1)S(1)}, bf16[1,32,64,512]{3,2,0,1:T(8,128)(2,1)S(1)}, u32[]{:S(2)}, u32[]{:S(2)}) %collective-permute-start.29) | collective-permute-done | bytes 2097184 | tf_op jit(solution)/shard_map/ppermute | solution.py:53
  1653.8 35.4 %collective-permute-done.30 = bf16[1,32,64,512]{3,2,0,1:T(8,128)(2,1)} collective-permute-done((bf16[1,32,64,512]{3,2,0,1:T(8,128)(2,1)}, bf16[1,32,64,512]{3,2,0,1:T(8,128)(2,1)}, u32[]{:S(2)}, u32[]{:S(2)}) %collective-permute-start.30) | collective-permute-done | bytes 2097184 | tf_op jit(solution)/shard_map/ppermute | solution.py:53
  1695.5 91.1 %collective-permute-done.32 = bf16[1,32,64,512]{3,2,0,1:T(8,128)(2,1)} collective-permute-done((bf16[1,32,64,512]{3,2,0,1:T(8,128)(2,1)}, bf16[1,32,64,512]{3,2,0,1:T(8,128)(2,1)}, u32[]{:S(2)}, u32[]{:S(2)}) %collective-permute-start.32) | collective-permute-done | bytes 2097184 | tf_op jit(solution)/shard_map/ppermute | solution.py:53
  1807.0 86.3 %all-to-all-start.4 = ((bf16[8,2,64,512]{3,1,2,0:T(2,128)(2,1)}), bf16[8,2,64,512]{3,1,2,0:T(2,128)(2,1)S(1)}, u32[]{:S(2)}, u32[]{:S(2)}) async-start(bf16[8,2,64,512]{3,1,2,0:T(2,128)(2,1)} %copy.105), calls=%async_computation.4 | async-start | bytes 2097152 | tf_op jit(solution)/shard_map/all_to_all | solution.py:62
  1893.3 15.5 fusion.8
  1908.8 8.6 all-to-all-done.4
  1917.3 4.8 all-to-all-start.3
  1922.2 44.2 %bitcast_convert_fusion = bf16[2048,512]{1,0:T(8,128)(2,1)S(1)} fusion(bf16[32,512,512]{2,1,0:T(8,128)(2,1)} %bitcast.190, bf16[32,512,512]{2,1,0:T(8,128)(2,1)} %bitcast.197, bf16[16,512,2048]{2,1,0:T(8,128)(2,1)} %all-gather.18.cloned.1.call-done, bf16[16,512,2048]{2,1,0:T(8,128)(2,1)} %all-gather.16.cloned.1.call-done), kind=kOutput, calls=%fused_computation.51 | convolution fusion | flops 34453061632 | bytes 102760448 | tf_op jit(solution)/shard_map/te,tc->ec/dot_general | solution.py:159
  1969.2 25.0 %collective-permute-done.39 = bf16[4,256,512]{2,1,0:T(8,128)(2,1)} collective-permute-done((bf16[4,256,512]{2,1,0:T(8,128)(2,1)}, bf16[4,256,512]{2,1,0:T(8,128)(2,1)}, u32[]{:S(2)}, u32[]{:S(2)}) %collective-permute-start.39) | collective-permute-done | bytes 1048608 | tf_op jit(solution)/shard_map/ppermute | solution.py:43
  1999.3 11.9 collective-permute-done.40
  2023.9 25.4 %fusion.5 = bf16[32,512,512]{2,1,0:T(8,128)(2,1)} fusion(bf16[32,512,512]{2,1,0:T(8,128)(2,1)} %bitcast.191, bf16[16,512,512]{2,1,0:T(8,128)(2,1)} %multiply_convert_fusion, bf16[16,512,512]{2,1,0:T(8,128)(2,1)} %multiply_convert_fusion.1, bf16[32,512,512]{2,1,0:T(8,128)(2,1)} %bitcast.198), kind=kLoop, calls=%fused_computation.7 | loop fusion | flops 92274688 | bytes 67108864 | tf_op jit(solution)/shard_map/convert_element_type | solution.py:156
  2054.5 17.3 fusion.18
  2071.8 11.1 dynamic_update_slice.141
  2082.9 6.1 convert_dynamic-update-slice_fusion
  2089.0 4.6 convert_dynamic-update-slice_fusion.1
  2096.8 4.2 dynamic_update_slice.173
  (256 shorter events, 185.4 us)
Async XLA Ops:
  7.2 213.7 %copy-start = (bf16[2048,512]{1,0:T(8,128)(2,1)S(1)}, bf16[2048,512]{1,0:T(8,128)(2,1)}, u32[]{:S(2)}) copy-start(bf16[2048,512]{1,0:T(8,128)(2,1)} %param.12) | copy-start | bytes 6291460
  7.2 213.7 %all-gather.16.cloned.1.call-start = ((), (), s32[]{:S(2)}) async-start(), calls=%async_computation.13 | async-start | bytes 41943040 | tf_op jit(solution)/shard_map/all_gather | solution.py:113
  19.0 405.0 %all-gather.18.cloned.1.call-start = ((), (), s32[]{:S(2)}) async-start(), calls=%async_computation.14 | async-start | bytes 41943040 | tf_op jit(solution)/shard_map/all_gather | solution.py:113
  19.7 619.6 %all-gather.20.cloned.1.call-start = ((), (), s32[]{:S(2)}) async-start(), calls=%async_computation.15 | async-start | bytes 10485760 | tf_op jit(solution)/shard_map/all_gather | solution.py:126
  259.7 350.3 %all-to-all-start = ((bf16[8,16,64,512]{3,2,1,0:T(8,128)(2,1)}), bf16[8,16,64,512]{3,2,1,0:T(8,128)(2,1)}, u32[]{:S(2)}, u32[]{:S(2)}) async-start(bf16[8,16,64,512]{3,2,1,0:T(8,128)(2,1)} %bitcast.199), calls=%async_computation | async-start | bytes 16777216 | tf_op jit(solution)/shard_map/all_to_all | solution.py:62
  265.8 697.4 %all-gather.8.cloned.1.call-start = ((), (), s32[]{:S(2)}) async-start(), calls=%async_computation.9 | async-start | bytes 1310720 | tf_op jit(solution)/shard_map/all_gather | solution.py:101
  267.5 709.4 %all-gather.10.cloned.1.call-start = ((), (), s32[]{:S(2)}) async-start(), calls=%async_computation.10 | async-start | bytes 2621440 | tf_op jit(solution)/shard_map/all_gather | solution.py:101
  269.5 718.1 %all-gather.12.cloned.1.call-start = ((), (), s32[]{:S(2)}) async-start(), calls=%async_computation.11 | async-start | bytes 5242880 | tf_op jit(solution)/shard_map/all_gather | solution.py:101
  457.4 25.5 %collective-permute-start = (bf16[1,16,64,512]{3,2,1,0:T(8,128)(2,1)}, bf16[1,16,64,512]{3,2,1,0:T(8,128)(2,1)}, u32[]{:S(2)}, u32[]{:S(2)}) collective-permute-start(bf16[1,16,64,512]{3,2,1,0:T(8,128)(2,1)} %get-tuple-element.41), channel_id=1, source_target_pairs={{0,4},{4,0},{8,12},{12,8},{16,20},{20,16},{24,28},{28,24},{1,5},{5... | collective-permute-start | bytes 3145736 | tf_op jit(solution)/shard_map/ppermute | solution.py:53
  458.1 67.4 %collective-permute-start.1 = (bf16[1,16,64,512]{3,2,1,0:T(8,128)(2,1)}, bf16[1,16,64,512]{3,2,1,0:T(8,128)(2,1)}, u32[]{:S(2)}, u32[]{:S(2)}) collective-permute-start(bf16[1,16,64,512]{3,2,1,0:T(8,128)(2,1)} %get-tuple-element.40), channel_id=1, source_target_pairs={{0,8},{4,12},{8,0},{12,4},{16,24},{20,28},{24,16},{28,20},{1,9},{5... | collective-permute-start | bytes 3145736 | tf_op jit(solution)/shard_map/ppermute | solution.py:53
  461.9 86.4 %collective-permute-start.2 = (bf16[1,16,64,512]{3,2,1,0:T(8,128)(2,1)}, bf16[1,16,64,512]{3,2,1,0:T(8,128)(2,1)}, u32[]{:S(2)}, u32[]{:S(2)}) collective-permute-start(bf16[1,16,64,512]{3,2,1,0:T(8,128)(2,1)} %get-tuple-element.39), channel_id=1, source_target_pairs={{0,12},{4,8},{8,4},{12,0},{16,28},{20,24},{24,20},{28,16},{1,13},{... | collective-permute-start | bytes 3145736 | tf_op jit(solution)/shard_map/ppermute | solution.py:53
  463.4 87.2 %collective-permute-start.3 = (bf16[1,16,64,512]{3,2,1,0:T(8,128)(2,1)}, bf16[1,16,64,512]{3,2,1,0:T(8,128)(2,1)}, u32[]{:S(2)}, u32[]{:S(2)}) collective-permute-start(bf16[1,16,64,512]{3,2,1,0:T(8,128)(2,1)} %get-tuple-element.38), channel_id=1, source_target_pairs={{0,16},{4,20},{8,24},{12,28},{16,0},{20,4},{24,8},{28,12},{1,17},{... | collective-permute-start | bytes 3145736 | tf_op jit(solution)/shard_map/ppermute | solution.py:53
  466.2 137.0 %collective-permute-start.4 = (bf16[1,16,64,512]{3,2,1,0:T(8,128)(2,1)}, bf16[1,16,64,512]{3,2,1,0:T(8,128)(2,1)}, u32[]{:S(2)}, u32[]{:S(2)}) collective-permute-start(bf16[1,16,64,512]{3,2,1,0:T(8,128)(2,1)} %get-tuple-element.37), channel_id=1, source_target_pairs={{0,20},{4,16},{8,28},{12,24},{16,4},{20,0},{24,12},{28,8},{1,21},{... | collective-permute-start | bytes 3145736 | tf_op jit(solution)/shard_map/ppermute | solution.py:53
  482.9 122.6 %collective-permute-start.5 = (bf16[1,16,64,512]{3,2,1,0:T(8,128)(2,1)S(1)}, bf16[1,16,64,512]{3,2,1,0:T(8,128)(2,1)}, u32[]{:S(2)}, u32[]{:S(2)}) collective-permute-start(bf16[1,16,64,512]{3,2,1,0:T(8,128)(2,1)S(1)} %get-tuple-element.36), channel_id=1, source_target_pairs={{0,24},{4,28},{8,16},{12,20},{16,8},{20,12},{24,0},{28,4},{1,25},{... | collective-permute-start | bytes 3145736 | tf_op jit(solution)/shard_map/ppermute | solution.py:53
  525.6 82.2 %collective-permute-start.6 = (bf16[1,16,64,512]{3,2,1,0:T(8,128)(2,1)S(1)}, bf16[1,16,64,512]{3,2,1,0:T(8,128)(2,1)}, u32[]{:S(2)}, u32[]{:S(2)}) collective-permute-start(bf16[1,16,64,512]{3,2,1,0:T(8,128)(2,1)S(1)} %get-tuple-element.35), channel_id=1, source_target_pairs={{0,28},{4,24},{8,20},{12,16},{16,12},{20,8},{24,4},{28,0},{1,29},{... | collective-permute-start | bytes 3145736 | tf_op jit(solution)/shard_map/ppermute | solution.py:53
  681.7 247.8 %all-to-all-start.1 = ((bf16[8,18,64,512]{3,2,1,0:T(8,128)(2,1)}), bf16[8,18,64,512]{3,2,1,0:T(8,128)(2,1)}, u32[]{:S(2)}, u32[]{:S(2)}) async-start(bf16[8,18,64,512]{3,2,1,0:T(8,128)(2,1)} %copy.102), calls=%async_computation.1 | async-start | bytes 18874368 | tf_op jit(solution)/shard_map/all_to_all | solution.py:62
  725.4 290.7 %all-gather.14.cloned.1.call-start = ((), (), s32[]{:S(2)}) async-start(), calls=%async_computation.12 | async-start | bytes 11796480 | tf_op jit(solution)/shard_map/all_gather | solution.py:101
  728.9 1367.9 %reduce-scatter.4.cloned.1.call-start = ((), (), s32[]{:S(2)}) async-start(), calls=%async_computation.16 | async-start | bytes 11796480 | tf_op jit(solution)/shard_map/reduce_scatter | solution.py:180
  729.0 209.1 %copy-start.26 = (pred[18,512]{1,0:T(8,128)(4,1)}, pred[18,512]{1,0:T(8,128)(4,1)S(1)}, u32[]{:S(2)}) copy-start(pred[18,512]{1,0:T(8,128)(4,1)S(1)} %get-tuple-element.67) | copy-start | bytes 27652
  952.0 457.6 %copy-start.29 = (pred[8,512]{1,0:T(8,128)(4,1)}, pred[8,512]{1,0:T(8,128)(4,1)S(1)}, u32[]{:S(2)}) copy-start(pred[8,512]{1,0:T(8,128)(4,1)S(1)} %get-tuple-element.65) | copy-start | bytes 12292
  966.6 35.4 %all-to-all-start.5 = ((bf16[8,2,64,512]{3,2,1,0:T(8,128)(2,1)}), bf16[8,2,64,512]{3,2,1,0:T(8,128)(2,1)S(1)}, u32[]{:S(2)}, u32[]{:S(2)}) async-start(bf16[8,2,64,512]{3,2,1,0:T(8,128)(2,1)} %bitcast.188), calls=%async_computation.5 | async-start | bytes 2097152 | tf_op jit(solution)/shard_map/all_to_all | solution.py:62
  981.7 30.6 %collective-permute-start.7 = (bf16[1,4,64,512]{3,2,0,1:T(8,128)(2,1)}, bf16[1,4,64,512]{3,2,0,1:T(8,128)(2,1)}, u32[]{:S(2)}, u32[]{:S(2)}) collective-permute-start(bf16[1,4,64,512]{3,2,0,1:T(8,128)(2,1)} %get-tuple-element.57), channel_id=1, source_target_pairs={{0,4},{4,0},{8,12},{12,8},{16,20},{20,16},{24,28},{28,24},{1,5},{5... | collective-permute-start | bytes 786440 | tf_op jit(solution)/shard_map/ppermute | solution.py:53
  981.7 33.9 %collective-permute-start.8 = (bf16[1,4,64,512]{3,2,0,1:T(8,128)(2,1)}, bf16[1,4,64,512]{3,2,0,1:T(8,128)(2,1)}, u32[]{:S(2)}, u32[]{:S(2)}) collective-permute-start(bf16[1,4,64,512]{3,2,0,1:T(8,128)(2,1)} %get-tuple-element.56), channel_id=1, source_target_pairs={{0,8},{4,12},{8,0},{12,4},{16,24},{20,28},{24,16},{28,20},{1,9},{5... | collective-permute-start | bytes 786440 | tf_op jit(solution)/shard_map/ppermute | solution.py:53
  983.7 32.4 %collective-permute-start.9 = (bf16[1,4,64,512]{3,2,0,1:T(8,128)(2,1)}, bf16[1,4,64,512]{3,2,0,1:T(8,128)(2,1)}, u32[]{:S(2)}, u32[]{:S(2)}) collective-permute-start(bf16[1,4,64,512]{3,2,0,1:T(8,128)(2,1)} %get-tuple-element.55), channel_id=1, source_target_pairs={{0,12},{4,8},{8,4},{12,0},{16,28},{20,24},{24,20},{28,16},{1,13},{... | collective-permute-start | bytes 786440 | tf_op jit(solution)/shard_map/ppermute | solution.py:53
  985.2 44.0 %collective-permute-start.10 = (bf16[1,4,64,512]{3,2,0,1:T(8,128)(2,1)}, bf16[1,4,64,512]{3,2,0,1:T(8,128)(2,1)}, u32[]{:S(2)}, u32[]{:S(2)}) collective-permute-start(bf16[1,4,64,512]{3,2,0,1:T(8,128)(2,1)} %get-tuple-element.54), channel_id=1, source_target_pairs={{0,16},{4,20},{8,24},{12,28},{16,0},{20,4},{24,8},{28,12},{1,17},{... | collective-permute-start | bytes 786440 | tf_op jit(solution)/shard_map/ppermute | solution.py:53
  987.5 43.6 %collective-permute-start.11 = (bf16[1,4,64,512]{3,2,0,1:T(8,128)(2,1)}, bf16[1,4,64,512]{3,2,0,1:T(8,128)(2,1)S(1)}, u32[]{:S(2)}, u32[]{:S(2)}) collective-permute-start(bf16[1,4,64,512]{3,2,0,1:T(8,128)(2,1)} %get-tuple-element.53), channel_id=1, source_target_pairs={{0,20},{4,16},{8,28},{12,24},{16,4},{20,0},{24,12},{28,8},{1,21},{... | collective-permute-start | bytes 786440 | tf_op jit(solution)/shard_map/ppermute | solution.py:53
  1002.0 403.8 %all-to-all-start.2 = ((bf16[8,8,64,512]{3,1,2,0:T(8,128)(2,1)}), bf16[8,8,64,512]{3,1,2,0:T(8,128)(2,1)}, u32[]{:S(2)}, u32[]{:S(2)}) async-start(bf16[8,8,64,512]{3,1,2,0:T(8,128)(2,1)} %copy.103), calls=%async_computation.2 | async-start | bytes 8388608 | tf_op jit(solution)/shard_map/all_to_all | solution.py:62
  1008.4 1092.6 %reduce-scatter.6.cloned.1.call-start = ((), (), s32[]{:S(2)}) async-start(), calls=%async_computation.17 | async-start | bytes 5242880 | tf_op jit(solution)/shard_map/reduce_scatter | solution.py:180
  1012.3 77.4 %collective-permute-start.12 = (bf16[1,4,64,512]{3,2,0,1:T(8,128)(2,1)}, bf16[1,4,64,512]{3,2,0,1:T(8,128)(2,1)}, u32[]{:S(2)}, u32[]{:S(2)}) collective-permute-start(bf16[1,4,64,512]{3,2,0,1:T(8,128)(2,1)} %get-tuple-element.52), channel_id=1, source_target_pairs={{0,24},{4,28},{8,16},{12,20},{16,8},{20,12},{24,0},{28,4},{1,25},{... | collective-permute-start | bytes 786440 | tf_op jit(solution)/shard_map/ppermute | solution.py:53
  1015.5 121.3 %collective-permute-start.14 = (bf16[1,8,64,512]{3,2,0,1:T(8,128)(2,1)}, bf16[1,8,64,512]{3,2,0,1:T(8,128)(2,1)}, u32[]{:S(2)}, u32[]{:S(2)}) collective-permute-start(bf16[1,8,64,512]{3,2,0,1:T(8,128)(2,1)} %get-tuple-element.48), channel_id=1, source_target_pairs={{0,4},{4,0},{8,12},{12,8},{16,20},{20,16},{24,28},{28,24},{1,5},{5... | collective-permute-start | bytes 1572872 | tf_op jit(solution)/shard_map/ppermute | solution.py:53
  1016.1 130.3 %collective-permute-start.15 = (bf16[1,8,64,512]{3,2,0,1:T(8,128)(2,1)}, bf16[1,8,64,512]{3,2,0,1:T(8,128)(2,1)}, u32[]{:S(2)}, u32[]{:S(2)}) collective-permute-start(bf16[1,8,64,512]{3,2,0,1:T(8,128)(2,1)} %get-tuple-element.47), channel_id=1, source_target_pairs={{0,8},{4,12},{8,0},{12,4},{16,24},{20,28},{24,16},{28,20},{1,9},{5... | collective-permute-start | bytes 1572872 | tf_op jit(solution)/shard_map/ppermute | solution.py:53
  1029.2 105.7 %collective-permute-start.13 = (bf16[1,4,64,512]{3,2,0,1:T(8,128)(2,1)S(1)}, bf16[1,4,64,512]{3,2,0,1:T(8,128)(2,1)S(1)}, u32[]{:S(2)}, u32[]{:S(2)}) collective-permute-start(bf16[1,4,64,512]{3,2,0,1:T(8,128)(2,1)S(1)} %copy-done.25), channel_id=1, source_target_pairs={{0,28},{4,24},{8,20},{12,16},{16,12},{20,8},{24,4},{28,0},{1,29},{... | collective-permute-start | bytes 786440 | tf_op jit(solution)/shard_map/ppermute | solution.py:53
  1031.1 116.9 %collective-permute-start.16 = (bf16[1,8,64,512]{3,2,0,1:T(8,128)(2,1)S(1)}, bf16[1,8,64,512]{3,2,0,1:T(8,128)(2,1)S(1)}, u32[]{:S(2)}, u32[]{:S(2)}) collective-permute-start(bf16[1,8,64,512]{3,2,0,1:T(8,128)(2,1)S(1)} %copy-done.22), channel_id=1, source_target_pairs={{0,12},{4,8},{8,4},{12,0},{16,28},{20,24},{24,20},{28,16},{1,13},{... | collective-permute-start | bytes 1572872 | tf_op jit(solution)/shard_map/ppermute | solution.py:53
  1089.6 76.8 %collective-permute-start.17 = (bf16[1,8,64,512]{3,2,0,1:T(8,128)(2,1)S(1)}, bf16[1,8,64,512]{3,2,0,1:T(8,128)(2,1)S(1)}, u32[]{:S(2)}, u32[]{:S(2)}) collective-permute-start(bf16[1,8,64,512]{3,2,0,1:T(8,128)(2,1)S(1)} %copy-done.21), channel_id=1, source_target_pairs={{0,16},{4,20},{8,24},{12,28},{16,0},{20,4},{24,8},{28,12},{1,17},{... | collective-permute-start | bytes 1572872 | tf_op jit(solution)/shard_map/ppermute | solution.py:53
  1127.7 110.8 %slice-start = ((s8[9437184]{0:T(1024)(128)(4,1)}), s8[1048576]{0:T(1024)(128)(4,1)S(1)}, s32[]{:S(2)}) async-start(s8[9437184]{0:T(1024)(128)(4,1)} %bitcast.205), calls=%async_computation.19 | async-start | bytes 2097152
  1127.8 110.8 %slice-start.1 = ((s8[9437184]{0:T(1024)(128)(4,1)}), s8[4194304]{0:T(1024)(128)(4,1)S(1)}, s32[]{:S(2)}) async-start(s8[9437184]{0:T(1024)(128)(4,1)} %bitcast.205), calls=%async_computation.20 | async-start | bytes 8388608
  1134.9 101.3 %collective-permute-start.21 = (bf16[1,18,64,512]{3,2,0,1:T(8,128)(2,1)S(1)}, bf16[1,18,64,512]{3,2,0,1:T(8,128)(2,1)S(1)}, u32[]{:S(2)}, u32[]{:S(2)}) collective-permute-start(bf16[1,18,64,512]{3,2,0,1:T(8,128)(2,1)S(1)} %get-tuple-element.34), channel_id=1, source_target_pairs={{0,4},{4,0},{8,12},{12,8},{16,20},{20,16},{24,28},{28,24},{1,5},{5... | collective-permute-start | bytes 3538952 | tf_op jit(solution)/shard_map/ppermute | solution.py:53
  1136.8 41.9 %collective-permute-start.18 = (bf16[1,8,64,512]{3,2,0,1:T(8,128)(2,1)S(1)}, bf16[1,8,64,512]{3,2,0,1:T(8,128)(2,1)S(1)}, u32[]{:S(2)}, u32[]{:S(2)}) collective-permute-start(bf16[1,8,64,512]{3,2,0,1:T(8,128)(2,1)S(1)} %copy-done.20), channel_id=1, source_target_pairs={{0,20},{4,16},{8,28},{12,24},{16,4},{20,0},{24,12},{28,8},{1,21},{... | collective-permute-start | bytes 1572872 | tf_op jit(solution)/shard_map/ppermute | solution.py:53
  1146.4 91.8 %collective-permute-start.22 = (bf16[1,18,64,512]{3,2,0,1:T(8,128)(2,1)}, bf16[1,18,64,512]{3,2,0,1:T(8,128)(2,1)S(1)}, u32[]{:S(2)}, u32[]{:S(2)}) collective-permute-start(bf16[1,18,64,512]{3,2,0,1:T(8,128)(2,1)} %get-tuple-element.33), channel_id=1, source_target_pairs={{0,8},{4,12},{8,0},{12,4},{16,24},{20,28},{24,16},{28,20},{1,9},{5... | collective-permute-start | bytes 3538952 | tf_op jit(solution)/shard_map/ppermute | solution.py:53
  1148.0 51.7 %collective-permute-start.19 = (bf16[1,8,64,512]{3,2,0,1:T(8,128)(2,1)S(1)}, bf16[1,8,64,512]{3,2,0,1:T(8,128)(2,1)S(1)}, u32[]{:S(2)}, u32[]{:S(2)}) collective-permute-start(bf16[1,8,64,512]{3,2,0,1:T(8,128)(2,1)S(1)} %copy-done.19), channel_id=1, source_target_pairs={{0,24},{4,28},{8,16},{12,20},{16,8},{20,12},{24,0},{28,4},{1,25},{... | collective-permute-start | bytes 1572872 | tf_op jit(solution)/shard_map/ppermute | solution.py:53
  1166.5 47.7 %collective-permute-start.20 = (bf16[1,8,64,512]{3,2,0,1:T(8,128)(2,1)S(1)}, bf16[1,8,64,512]{3,2,0,1:T(8,128)(2,1)S(1)}, u32[]{:S(2)}, u32[]{:S(2)}) collective-permute-start(bf16[1,8,64,512]{3,2,0,1:T(8,128)(2,1)S(1)} %copy-done.18), channel_id=1, source_target_pairs={{0,28},{4,24},{8,20},{12,16},{16,12},{20,8},{24,4},{28,0},{1,29},{... | collective-permute-start | bytes 1572872 | tf_op jit(solution)/shard_map/ppermute | solution.py:53
  1178.7 75.5 %collective-permute-start.23 = (bf16[1,18,64,512]{3,2,0,1:T(8,128)(2,1)}, bf16[1,18,64,512]{3,2,0,1:T(8,128)(2,1)S(1)}, u32[]{:S(2)}, u32[]{:S(2)}) collective-permute-start(bf16[1,18,64,512]{3,2,0,1:T(8,128)(2,1)} %get-tuple-element.32), channel_id=1, source_target_pairs={{0,12},{4,8},{8,4},{12,0},{16,28},{20,24},{24,20},{28,16},{1,13},{... | collective-permute-start | bytes 3538952 | tf_op jit(solution)/shard_map/ppermute | solution.py:53
  1199.8 157.9 %collective-permute-start.24 = (bf16[1,18,64,512]{3,2,0,1:T(8,128)(2,1)}, bf16[1,18,64,512]{3,2,0,1:T(8,128)(2,1)S(1)}, u32[]{:S(2)}, u32[]{:S(2)}) collective-permute-start(bf16[1,18,64,512]{3,2,0,1:T(8,128)(2,1)} %get-tuple-element.31), channel_id=1, source_target_pairs={{0,16},{4,20},{8,24},{12,28},{16,0},{20,4},{24,8},{28,12},{1,17},{... | collective-permute-start | bytes 3538952 | tf_op jit(solution)/shard_map/ppermute | solution.py:53
  1214.1 168.0 %collective-permute-start.25 = (bf16[1,18,64,512]{3,2,0,1:T(8,128)(2,1)}, bf16[1,18,64,512]{3,2,0,1:T(8,128)(2,1)S(1)}, u32[]{:S(2)}, u32[]{:S(2)}) collective-permute-start(bf16[1,18,64,512]{3,2,0,1:T(8,128)(2,1)} %get-tuple-element.30), channel_id=1, source_target_pairs={{0,20},{4,16},{8,28},{12,24},{16,4},{20,0},{24,12},{28,8},{1,21},{... | collective-permute-start | bytes 3538952 | tf_op jit(solution)/shard_map/ppermute | solution.py:53
  1236.3 146.0 %collective-permute-start.26 = (bf16[1,18,64,512]{3,2,0,1:T(8,128)(2,1)}, bf16[1,18,64,512]{3,2,0,1:T(8,128)(2,1)S(1)}, u32[]{:S(2)}, u32[]{:S(2)}) collective-permute-start(bf16[1,18,64,512]{3,2,0,1:T(8,128)(2,1)} %get-tuple-element.29), channel_id=1, source_target_pairs={{0,24},{4,28},{8,16},{12,20},{16,8},{20,12},{24,0},{28,4},{1,25},{... | collective-permute-start | bytes 3538952 | tf_op jit(solution)/shard_map/ppermute | solution.py:53
  1238.3 144.2 %collective-permute-start.27 = (bf16[1,18,64,512]{3,2,0,1:T(8,128)(2,1)}, bf16[1,18,64,512]{3,2,0,1:T(8,128)(2,1)S(1)}, u32[]{:S(2)}, u32[]{:S(2)}) collective-permute-start(bf16[1,18,64,512]{3,2,0,1:T(8,128)(2,1)} %get-tuple-element.28), channel_id=1, source_target_pairs={{0,28},{4,24},{8,20},{12,16},{16,12},{20,8},{24,4},{28,0},{1,29},{... | collective-permute-start | bytes 3538952 | tf_op jit(solution)/shard_map/ppermute | solution.py:53
  1456.7 58.4 %collective-permute-start.28 = (bf16[1,32,64,512]{3,2,0,1:T(8,128)(2,1)S(1)}, bf16[1,32,64,512]{3,2,0,1:T(8,128)(2,1)S(1)}, u32[]{:S(2)}, u32[]{:S(2)}) collective-permute-start(bf16[1,32,64,512]{3,2,0,1:T(8,128)(2,1)S(1)} %get-tuple-element.23), channel_id=1, source_target_pairs={{0,4},{4,0},{8,12},{12,8},{16,20},{20,16},{24,28},{28,24},{1,5},{5... | collective-permute-start | bytes 6291464 | tf_op jit(solution)/shard_map/ppermute | solution.py:53
  1459.0 186.3 %collective-permute-start.29 = (bf16[1,32,64,512]{3,2,0,1:T(8,128)(2,1)S(1)}, bf16[1,32,64,512]{3,2,0,1:T(8,128)(2,1)S(1)}, u32[]{:S(2)}, u32[]{:S(2)}) collective-permute-start(bf16[1,32,64,512]{3,2,0,1:T(8,128)(2,1)S(1)} %get-tuple-element.22), channel_id=1, source_target_pairs={{0,8},{4,12},{8,0},{12,4},{16,24},{20,28},{24,16},{28,20},{1,9},{5... | collective-permute-start | bytes 6291464 | tf_op jit(solution)/shard_map/ppermute | solution.py:53
  1509.6 179.6 %collective-permute-start.30 = (bf16[1,32,64,512]{3,2,0,1:T(8,128)(2,1)}, bf16[1,32,64,512]{3,2,0,1:T(8,128)(2,1)}, u32[]{:S(2)}, u32[]{:S(2)}) collective-permute-start(bf16[1,32,64,512]{3,2,0,1:T(8,128)(2,1)} %get-tuple-element.21), channel_id=1, source_target_pairs={{0,12},{4,8},{8,4},{12,0},{16,28},{20,24},{24,20},{28,16},{1,13},{... | collective-permute-start | bytes 6291464 | tf_op jit(solution)/shard_map/ppermute | solution.py:53
  1510.3 182.0 %collective-permute-start.31 = (bf16[1,32,64,512]{3,2,0,1:T(8,128)(2,1)}, bf16[1,32,64,512]{3,2,0,1:T(8,128)(2,1)}, u32[]{:S(2)}, u32[]{:S(2)}) collective-permute-start(bf16[1,32,64,512]{3,2,0,1:T(8,128)(2,1)} %get-tuple-element.20), channel_id=1, source_target_pairs={{0,16},{4,20},{8,24},{12,28},{16,0},{20,4},{24,8},{28,12},{1,17},{... | collective-permute-start | bytes 6291464 | tf_op jit(solution)/shard_map/ppermute | solution.py:53
  1513.6 273.0 %collective-permute-start.32 = (bf16[1,32,64,512]{3,2,0,1:T(8,128)(2,1)}, bf16[1,32,64,512]{3,2,0,1:T(8,128)(2,1)}, u32[]{:S(2)}, u32[]{:S(2)}) collective-permute-start(bf16[1,32,64,512]{3,2,0,1:T(8,128)(2,1)} %get-tuple-element.19), channel_id=1, source_target_pairs={{0,20},{4,16},{8,28},{12,24},{16,4},{20,0},{24,12},{28,8},{1,21},{... | collective-permute-start | bytes 6291464 | tf_op jit(solution)/shard_map/ppermute | solution.py:53
  1515.1 130.2 %copy-start.10 = (bf16[1,32,64,512]{3,2,0,1:T(8,128)(2,1)}, bf16[1,32,64,512]{3,2,0,1:T(8,128)(2,1)S(1)}, u32[]{:S(2)}) copy-start(bf16[1,32,64,512]{3,2,0,1:T(8,128)(2,1)S(1)} %collective-permute-done.28) | copy-start | bytes 6291460
  1515.1 274.6 %collective-permute-start.33 = (bf16[1,32,64,512]{3,2,0,1:T(8,128)(2,1)}, bf16[1,32,64,512]{3,2,0,1:T(8,128)(2,1)}, u32[]{:S(2)}, u32[]{:S(2)}) collective-permute-start(bf16[1,32,64,512]{3,2,0,1:T(8,128)(2,1)} %get-tuple-element.18), channel_id=1, source_target_pairs={{0,24},{4,28},{8,16},{12,20},{16,8},{20,12},{24,0},{28,4},{1,25},{... | collective-permute-start | bytes 6291464 | tf_op jit(solution)/shard_map/ppermute | solution.py:53
  1646.7 146.2 %collective-permute-start.34 = (bf16[1,32,64,512]{3,2,0,1:T(8,128)(2,1)S(1)}, bf16[1,32,64,512]{3,2,0,1:T(8,128)(2,1)}, u32[]{:S(2)}, u32[]{:S(2)}) collective-permute-start(bf16[1,32,64,512]{3,2,0,1:T(8,128)(2,1)S(1)} %get-tuple-element.17), channel_id=1, source_target_pairs={{0,28},{4,24},{8,20},{12,16},{16,12},{20,8},{24,4},{28,0},{1,29},{... | collective-permute-start | bytes 6291464 | tf_op jit(solution)/shard_map/ppermute | solution.py:53
  1807.0 110.3 %all-to-all-start.4 = ((bf16[8,2,64,512]{3,1,2,0:T(2,128)(2,1)}), bf16[8,2,64,512]{3,1,2,0:T(2,128)(2,1)S(1)}, u32[]{:S(2)}, u32[]{:S(2)}) async-start(bf16[8,2,64,512]{3,1,2,0:T(2,128)(2,1)} %copy.105), calls=%async_computation.4 | async-start | bytes 2097152 | tf_op jit(solution)/shard_map/all_to_all | solution.py:62
  1893.3 213.7 %reduce-scatter.8.cloned.1.call-start = ((), (), s32[]{:S(2)}) async-start(), calls=%async_computation.18 | async-start | bytes 10485760 | tf_op jit(solution)/shard_map/reduce_scatter | solution.py:148
  1917.3 102.0 %all-to-all-start.3 = ((bf16[8,4,64,512]{3,1,2,0:T(4,128)(2,1)}), bf16[8,4,64,512]{3,1,2,0:T(4,128)(2,1)S(1)}, u32[]{:S(2)}, u32[]{:S(2)}) async-start(bf16[8,4,64,512]{3,1,2,0:T(4,128)(2,1)} %copy.104), calls=%async_computation.3 | async-start | bytes 4194304 | tf_op jit(solution)/shard_map/all_to_all | solution.py:62
  1968.8 25.5 %collective-permute-start.39 = (bf16[4,256,512]{2,1,0:T(8,128)(2,1)}, bf16[4,256,512]{2,1,0:T(8,128)(2,1)}, u32[]{:S(2)}, u32[]{:S(2)}) collective-permute-start(bf16[4,256,512]{2,1,0:T(8,128)(2,1)} %dynamic-slice_bitcast_fusion.7), channel_id=1, source_target_pairs={{0,4},{4,0},{8,12},{12,8},{16,20},{20,16},{24,28},{28,24},{1,5},{5... | collective-permute-start | bytes 3145736 | tf_op jit(solution)/shard_map/ppermute | solution.py:43
  1997.9 13.4 collective-permute-start.40
  2013.4 35.9 %collective-permute-start.41 = (bf16[1,256,512]{2,1,0:T(8,128)(2,1)S(1)}, bf16[1,256,512]{2,1,0:T(8,128)(2,1)}, u32[]{:S(2)}, u32[]{:S(2)}) collective-permute-start(bf16[1,256,512]{2,1,0:T(8,128)(2,1)S(1)} %constant_dynamic-slice_fusion.5), channel_id=1, source_target_pairs={{0,16},{4,20},{8,24},{12,28},{16,0},{20,4},{24,8},{28,12},{1,17},{... | collective-permute-start | bytes 786440 | tf_op jit(solution)/shard_map/ppermute | solution.py:43
  2019.4 31.7 %collective-permute-start.37 = (bf16[2,2,128,512]{3,2,0,1:T(8,128)(2,1)}, bf16[2,2,128,512]{3,2,0,1:T(8,128)(2,1)S(1)}, u32[]{:S(2)}, u32[]{:S(2)}) collective-permute-start(bf16[2,2,128,512]{3,2,0,1:T(8,128)(2,1)} %bitcast.189), channel_id=1, source_target_pairs={{0,1},{1,0},{2,3},{3,2},{4,5},{5,4},{6,7},{7,6},{8,9},{9,8},{10,11... | collective-permute-start | bytes 1572872 | tf_op jit(solution)/shard_map/ppermute | solution.py:43
  2023.3 28.1 %collective-permute-start.35 = (bf16[4,2,128,512]{3,2,0,1:T(8,128)(2,1)S(1)}, bf16[4,2,128,512]{3,2,0,1:T(8,128)(2,1)S(1)}, u32[]{:S(2)}, u32[]{:S(2)}) collective-permute-start(bf16[4,2,128,512]{3,2,0,1:T(8,128)(2,1)S(1)} %bitcast.242), channel_id=1, source_target_pairs={{0,1},{1,0},{2,3},{3,2},{4,5},{5,4},{6,7},{7,6},{8,9},{9,8},{10,11... | collective-permute-start | bytes 3145736 | tf_op jit(solution)/shard_map/ppermute | solution.py:43
  2051.2 54.0 %collective-permute-start.38 = (bf16[2,1,128,512]{3,2,0,1:T(8,128)(2,1)S(1)}, bf16[2,1,128,512]{3,2,0,1:T(8,128)(2,1)}, u32[]{:S(2)}, u32[]{:S(2)}) collective-permute-start(bf16[2,1,128,512]{3,2,0,1:T(8,128)(2,1)S(1)} %constant_dynamic-slice_fusion.6), channel_id=1, source_target_pairs={{0,2},{1,3},{2,0},{3,1},{4,6},{5,7},{6,4},{7,5},{8,10},{9,11},{10,... | collective-permute-start | bytes 786440 | tf_op jit(solution)/shard_map/ppermute | solution.py:43
  2052.6 50.7 %collective-permute-start.36 = (bf16[4,1,128,512]{3,2,0,1:T(8,128)(2,1)}, bf16[4,1,128,512]{3,2,0,1:T(8,128)(2,1)}, u32[]{:S(2)}, u32[]{:S(2)}) collective-permute-start(bf16[4,1,128,512]{3,2,0,1:T(8,128)(2,1)} %constant_dynamic-slice_fusion.10), channel_id=1, source_target_pairs={{0,2},{1,3},{2,0},{3,1},{4,6},{5,7},{6,4},{7,5},{8,10},{9,11},{10,... | collective-permute-start | bytes 1572872 | tf_op jit(solution)/shard_map/ppermute | solution.py:43
  (30 other events, 782.1 us)
Sparse Core Ops, SparseCore 0:
  19.1 201.7 all-gather.15
  222.4 201.4 all-gather.17
  425.6 58.2 all-gather.19
  485.8 16.6 all-gather.7
  504.0 22.5 all-gather.9
  528.0 34.4 all-gather.11
  729.0 64.1 all-gather.13
  950.9 75.4 reduce-scatter.3
  1415.7 94.2 reduce-scatter.5
  1908.9 71.3 reduce-scatter.7
